TPU v7x, 32 devices: a whole 2x2x4 slice. The times are simulated.
32 devices in a mesh: rep: 2 (over y), shard: 16 (over z, x, core).
Axes of the slice: x: 2, y: 2, z: 4, core: 2. Of those that a mesh axis runs over, the one named last changes fastest.
Arguments:
- inputs: bfloat16 [32, 1024, 512], P(('rep', 'shard')), may hold values from -6 to 6
- segment_ids: int32 [32, 1024], P(('rep', 'shard')), may hold values from 0 to 3, never falling along the last dimension, each value on 1 to 800 neighbouring positions
- w_query: bfloat16 [512, 512], P('shard'), may hold values from -0.25 to 0.25
- w_key: bfloat16 [512, 512], P('shard'), may hold values from -0.25 to 0.25
- w_value: bfloat16 [512, 512], P('shard'), may hold values from -0.25 to 0.25
- w_out: bfloat16 [512, 512], P('shard'), may hold values from -3 to 3
- w_up: bfloat16 [512, 2048], P('shard'), may hold values from -0.25 to 0.25
- w_down: bfloat16 [2048, 512], P('shard'), may hold values from -0.125 to 0.125
- b_up: bfloat16 [2048], P('shard'), may hold values from -3 to 3
- b_down: bfloat16 [512], P('shard'), may hold values from -2 to 2
- gain_attn: bfloat16 [512], P('shard'), may hold values from 0.5 to 1.5
- shift_attn: bfloat16 [512], P('shard'), may hold values from -2 to 2
- gain_ffn: bfloat16 [512], P('shard'), may hold values from 0.5 to 1.5
- shift_ffn: bfloat16 [512], P('shard'), may hold values from -2 to 2
- cotangent: bfloat16 [32, 1024, 512], P(('rep', 'shard')), may hold values from -6 to 6
Outputs:
- output: bfloat16 [32, 1024, 512], P(('rep', 'shard'))
- grad_inputs: float32 [32, 1024, 512], P(('rep', 'shard'))
- grad_w_query: float32 [512, 512], P('shard')
- grad_w_key: float32 [512, 512], P('shard')
- grad_w_value: float32 [512, 512], P('shard')
- grad_w_out: float32 [512, 512], P('shard')
- grad_w_up: float32 [512, 2048], P('shard')
- grad_w_down: float32 [2048, 512], P('shard')
- grad_b_up: float32 [2048], P('shard')
- grad_b_down: float32 [512], P('shard')
- grad_gain_attn: float32 [512], P('shard')
- grad_shift_attn: float32 [512], P('shard')
- grad_gain_ffn: float32 [512], P('shard')
- grad_shift_ffn: float32 [512], P('shard')
Inputs may be any that keep to these rules, and one draw needn't show every extreme that they name: `segment_ids`: within a sequence the ids never fall, each document is one run of equal ids, and the longest document has 800 tokens.
All inputs are finite; a program needn't handle non-finite values.
Results may differ from a plain program's by a relative error of at most 0.04.
Values may be sent and summed in bfloat16 or wider, within the bound.
A program may use at most 128 MiB of HBM per device.

v0:
```python
import jax
import jax.numpy as jnp
from jax import lax
from jax.sharding import PartitionSpec as P

HEADS = 8
HEAD_DIM = 64


epsilon = 1e-05


def layer_norm(hidden, gain, shift):
    centre = hidden - jnp.mean(hidden, axis=-1, keepdims=True)
    scale = lax.rsqrt(jnp.mean(centre * centre, axis=-1, keepdims=True) + epsilon)
    normal = centre * scale
    return (normal * gain + shift, normal, scale)


def norm_back(grad_out, normal, scale, gain):
    grad_normal = grad_out * gain
    grad_hidden = scale * (
        grad_normal
        - jnp.mean(grad_normal, axis=-1, keepdims=True)
        - normal * jnp.mean(grad_normal * normal, axis=-1, keepdims=True)
    )
    return (grad_hidden, jnp.sum(grad_out * normal, axis=0), jnp.sum(grad_out, axis=0))


def feature(values):
    return jax.nn.elu(values) + 1.0


def causal_visible(segments, offset, block_rows):
    length = segments.shape[0]
    query_pos = offset + jnp.arange(block_rows, dtype=jnp.int32)
    key_pos = jnp.arange(length, dtype=jnp.int32)
    query_seg = segments[offset : offset + block_rows]
    return (query_seg[:, None] == segments[None, :]) & (key_pos[None, :] <= query_pos[:, None])


def attend_forward(packed):
    query_feat, key_feat, values, segments = packed
    length = query_feat.shape[0]
    block_rows = min(512, length)
    contexts = []
    totals_all = []
    for offset in range(0, length, block_rows):
        visible = causal_visible(segments, offset, block_rows)
        scores = jnp.einsum(
            "qhd,khd->hqk",
            query_feat[offset : offset + block_rows],
            key_feat,
            preferred_element_type=jnp.float32,
        )
        masked = jnp.where(visible[None], scores, 0.0)
        totals = jnp.transpose(jnp.sum(masked, axis=-1))
        mixed = jnp.einsum(
            "hqk,khd->qhd", masked.astype(jnp.bfloat16), values, preferred_element_type=jnp.float32
        )
        contexts.append(mixed / totals[:, :, None])
        totals_all.append(totals)
    return (jnp.concatenate(contexts, axis=0), jnp.concatenate(totals_all, axis=0))


def attend_backward(packed):
    query_feat, key_feat, values, segments, grad_mixed, grad_totals = packed
    length = query_feat.shape[0]
    block_rows = min(512, length)
    query_parts = []
    grad_keys = jnp.zeros(key_feat.shape, jnp.float32)
    grad_values = jnp.zeros(values.shape, jnp.float32)
    for offset in range(0, length, block_rows):
        visible = causal_visible(segments, offset, block_rows)
        query_block = query_feat[offset : offset + block_rows]
        mixed_block = grad_mixed[offset : offset + block_rows]
        scores = jnp.einsum(
            "qhd,khd->hqk", query_block, key_feat, preferred_element_type=jnp.float32
        )
        rounded = jnp.where(visible[None], scores, 0.0).astype(jnp.bfloat16)
        grad_weights = jnp.einsum(
            "qhd,khd->hqk", mixed_block, values, preferred_element_type=jnp.float32
        )
        grad_weights = (
            grad_weights + jnp.transpose(grad_totals[offset : offset + block_rows])[:, :, None]
        ).astype(jnp.bfloat16)
        grad_scores = jnp.where(visible[None], grad_weights, jnp.zeros((), jnp.bfloat16))
        query_parts.append(
            jnp.einsum("hqk,khd->qhd", grad_scores, key_feat, preferred_element_type=jnp.float32)
        )
        grad_keys = grad_keys + jnp.einsum(
            "hqk,qhd->khd", grad_scores, query_block, preferred_element_type=jnp.float32
        )
        grad_values = grad_values + jnp.einsum(
            "hqk,qhd->khd", rounded, mixed_block, preferred_element_type=jnp.float32
        )
    return (jnp.concatenate(query_parts, axis=0), grad_keys, grad_values)


def on_device(
    inputs,
    segment_ids,
    w_query,
    w_key,
    w_value,
    w_out,
    w_up,
    w_down,
    b_up,
    b_down,
    gain_attn,
    shift_attn,
    gain_ffn,
    shift_ffn,
    cotangent,
):
    sequences, length, model_width = inputs.shape
    row_count = sequences * length
    full_query, full_key, full_value, full_out, gain_one, shift_one = (
        lax.all_gather(w_query, "shard", axis=0, tiled=True),
        lax.all_gather(w_key, "shard", axis=0, tiled=True),
        lax.all_gather(w_value, "shard", axis=0, tiled=True),
        lax.all_gather(w_out, "shard", axis=0, tiled=True),
        lax.all_gather(gain_attn, "shard", axis=0, tiled=True),
        lax.all_gather(shift_attn, "shard", axis=0, tiled=True),
    )
    hidden_in = inputs.reshape(row_count, model_width).astype(jnp.float32)
    normed_one, normal_one, scale_one = layer_norm(
        hidden_in, gain_one.astype(jnp.float32), shift_one.astype(jnp.float32)
    )
    normed_attn = normed_one.astype(jnp.bfloat16)
    queries = jnp.dot(normed_attn, full_query, preferred_element_type=jnp.float32)
    keys_raw = jnp.dot(normed_attn, full_key, preferred_element_type=jnp.float32)
    values = jnp.dot(normed_attn, full_value, preferred_element_type=jnp.float32).astype(
        jnp.bfloat16
    )
    query_feat, query_pull = jax.vjp(feature, queries)
    key_feat, key_pull = jax.vjp(feature, keys_raw)
    head_shape = (sequences, length, HEADS, HEAD_DIM)
    query_heads = query_feat.astype(jnp.bfloat16).reshape(head_shape)
    key_heads = key_feat.astype(jnp.bfloat16).reshape(head_shape)
    value_heads = values.reshape(head_shape)
    full_up, full_down, bias_up, bias_down, gain_two, shift_two = (
        lax.all_gather(w_up, "shard", axis=0, tiled=True),
        lax.all_gather(w_down, "shard", axis=0, tiled=True),
        lax.all_gather(b_up, "shard", axis=0, tiled=True),
        lax.all_gather(b_down, "shard", axis=0, tiled=True),
        lax.all_gather(gain_ffn, "shard", axis=0, tiled=True),
        lax.all_gather(shift_ffn, "shard", axis=0, tiled=True),
    )
    context, totals = lax.map(attend_forward, (query_heads, key_heads, value_heads, segment_ids))
    context_low = context.reshape(row_count, model_width).astype(jnp.bfloat16)
    after_attn = hidden_in + jnp.dot(context_low, full_out, preferred_element_type=jnp.float32)
    normed_two, normal_two, scale_two = layer_norm(
        after_attn, gain_two.astype(jnp.float32), shift_two.astype(jnp.float32)
    )
    normed_ffn = normed_two.astype(jnp.bfloat16)
    pre_act = jnp.dot(normed_ffn, full_up, preferred_element_type=jnp.float32) + bias_up.astype(
        jnp.float32
    )
    activated, gelu_pull = jax.vjp(jax.nn.gelu, pre_act)
    hidden = activated.astype(jnp.bfloat16)
    result = (
        after_attn
        + jnp.dot(hidden, full_down, preferred_element_type=jnp.float32)
        + bias_down.astype(jnp.float32)
    )
    output = result.astype(jnp.bfloat16).reshape(inputs.shape)
    full_up, full_down, bias_up, bias_down, gain_two, shift_two = (
        lax.all_gather(w_up, "shard", axis=0, tiled=True),
        lax.all_gather(w_down, "shard", axis=0, tiled=True),
        lax.all_gather(b_up, "shard", axis=0, tiled=True),
        lax.all_gather(b_down, "shard", axis=0, tiled=True),
        lax.all_gather(gain_ffn, "shard", axis=0, tiled=True),
        lax.all_gather(shift_ffn, "shard", axis=0, tiled=True),
    )
    upstream = cotangent.reshape(row_count, model_width)
    upstream_f = upstream.astype(jnp.float32)
    grad_down = jnp.einsum("tf,td->fd", hidden, upstream, preferred_element_type=jnp.float32)
    grad_bias_down = jnp.sum(upstream_f, axis=0)
    grad_hidden = jnp.einsum("td,fd->tf", upstream, full_down, preferred_element_type=jnp.float32)
    grad_pre = gelu_pull(grad_hidden)[0].astype(jnp.bfloat16)
    grad_bias_up = jnp.sum(grad_pre.astype(jnp.float32), axis=0)
    grad_up = jnp.einsum("td,tf->df", normed_ffn, grad_pre, preferred_element_type=jnp.float32)
    grad_normed_two = jnp.einsum("tf,df->td", grad_pre, full_up, preferred_element_type=jnp.float32)
    grad_part, grad_gain_two, grad_shift_two = norm_back(
        grad_normed_two, normal_two, scale_two, gain_two.astype(jnp.float32)
    )
    grad_after = upstream_f + grad_part
    full_query, full_key, full_value, full_out, gain_one, shift_one = (
        lax.all_gather(w_query, "shard", axis=0, tiled=True),
        lax.all_gather(w_key, "shard", axis=0, tiled=True),
        lax.all_gather(w_value, "shard", axis=0, tiled=True),
        lax.all_gather(w_out, "shard", axis=0, tiled=True),
        lax.all_gather(gain_attn, "shard", axis=0, tiled=True),
        lax.all_gather(shift_attn, "shard", axis=0, tiled=True),
    )
    grad_attn_out = grad_after.astype(jnp.bfloat16)
    grad_out = jnp.einsum(
        "td,te->de", context_low, grad_attn_out, preferred_element_type=jnp.float32
    )
    grad_context = jnp.einsum(
        "te,de->td", grad_attn_out, full_out, preferred_element_type=jnp.float32
    ).astype(jnp.bfloat16)
    grad_context = grad_context.astype(jnp.float32).reshape(head_shape)
    grad_totals = -jnp.sum(grad_context * context, axis=-1) / totals
    grad_mixed = (grad_context / totals[..., None]).astype(jnp.bfloat16)
    grad_qfeat, grad_kfeat, grad_vals = lax.map(
        attend_backward, (query_heads, key_heads, value_heads, segment_ids, grad_mixed, grad_totals)
    )
    grad_queries = query_pull(grad_qfeat.reshape(row_count, model_width))[0].astype(jnp.bfloat16)
    grad_keys = key_pull(grad_kfeat.reshape(row_count, model_width))[0].astype(jnp.bfloat16)
    grad_values = grad_vals.reshape(row_count, model_width).astype(jnp.bfloat16)
    grad_query_w = jnp.einsum(
        "td,te->de", normed_attn, grad_queries, preferred_element_type=jnp.float32
    )
    grad_key_w = jnp.einsum("td,te->de", normed_attn, grad_keys, preferred_element_type=jnp.float32)
    grad_value_w = jnp.einsum(
        "td,te->de", normed_attn, grad_values, preferred_element_type=jnp.float32
    )
    grad_normed_one = jnp.einsum(
        "te,de->td", grad_queries, full_query, preferred_element_type=jnp.float32
    )
    grad_normed_one = grad_normed_one + jnp.einsum(
        "te,de->td", grad_keys, full_key, preferred_element_type=jnp.float32
    )
    grad_normed_one = grad_normed_one + jnp.einsum(
        "te,de->td", grad_values, full_value, preferred_element_type=jnp.float32
    )
    grad_first, grad_gain_one, grad_shift_one = norm_back(
        grad_normed_one, normal_one, scale_one, gain_one.astype(jnp.float32)
    )
    grad_inputs = (grad_after + grad_first).reshape(inputs.shape)
    grouped = (
        lax.psum_scatter(
            grad_query_w.astype(jnp.bfloat16), "shard", scatter_dimension=0, tiled=True
        ).astype(jnp.float32),
        lax.psum_scatter(
            grad_key_w.astype(jnp.bfloat16), "shard", scatter_dimension=0, tiled=True
        ).astype(jnp.float32),
        lax.psum_scatter(
            grad_value_w.astype(jnp.bfloat16), "shard", scatter_dimension=0, tiled=True
        ).astype(jnp.float32),
        lax.psum_scatter(
            grad_out.astype(jnp.bfloat16), "shard", scatter_dimension=0, tiled=True
        ).astype(jnp.float32),
        lax.psum_scatter(
            grad_up.astype(jnp.bfloat16), "shard", scatter_dimension=0, tiled=True
        ).astype(jnp.float32),
        lax.psum_scatter(
            grad_down.astype(jnp.bfloat16), "shard", scatter_dimension=0, tiled=True
        ).astype(jnp.float32),
        lax.psum_scatter(
            grad_bias_up.astype(jnp.bfloat16), "shard", scatter_dimension=0, tiled=True
        ).astype(jnp.float32),
        lax.psum_scatter(
            grad_bias_down.astype(jnp.bfloat16), "shard", scatter_dimension=0, tiled=True
        ).astype(jnp.float32),
        lax.psum_scatter(
            grad_gain_one.astype(jnp.bfloat16), "shard", scatter_dimension=0, tiled=True
        ).astype(jnp.float32),
        lax.psum_scatter(
            grad_shift_one.astype(jnp.bfloat16), "shard", scatter_dimension=0, tiled=True
        ).astype(jnp.float32),
        lax.psum_scatter(
            grad_gain_two.astype(jnp.bfloat16), "shard", scatter_dimension=0, tiled=True
        ).astype(jnp.float32),
        lax.psum_scatter(
            grad_shift_two.astype(jnp.bfloat16), "shard", scatter_dimension=0, tiled=True
        ).astype(jnp.float32),
    )
    (
        part_q,
        part_k,
        part_v,
        part_o,
        part_up,
        part_down,
        part_bup,
        part_bdown,
        part_gone,
        part_sone,
        part_gtwo,
        part_stwo,
    ) = grouped
    (
        owned_q,
        owned_k,
        owned_v,
        owned_o,
        owned_up,
        owned_down,
        owned_bup,
        owned_bdown,
        owned_gone,
        owned_sone,
        owned_gtwo,
        owned_stwo,
    ) = (
        lax.psum(part_q.astype(jnp.bfloat16), "rep").astype(jnp.float32),
        lax.psum(part_k.astype(jnp.bfloat16), "rep").astype(jnp.float32),
        lax.psum(part_v.astype(jnp.bfloat16), "rep").astype(jnp.float32),
        lax.psum(part_o.astype(jnp.bfloat16), "rep").astype(jnp.float32),
        lax.psum(part_up.astype(jnp.bfloat16), "rep").astype(jnp.float32),
        lax.psum(part_down.astype(jnp.bfloat16), "rep").astype(jnp.float32),
        lax.psum(part_bup.astype(jnp.bfloat16), "rep").astype(jnp.float32),
        lax.psum(part_bdown.astype(jnp.bfloat16), "rep").astype(jnp.float32),
        lax.psum(part_gone.astype(jnp.bfloat16), "rep").astype(jnp.float32),
        lax.psum(part_sone.astype(jnp.bfloat16), "rep").astype(jnp.float32),
        lax.psum(part_gtwo.astype(jnp.bfloat16), "rep").astype(jnp.float32),
        lax.psum(part_stwo.astype(jnp.bfloat16), "rep").astype(jnp.float32),
    )
    return (
        output,
        grad_inputs,
        owned_q,
        owned_k,
        owned_v,
        owned_o,
        owned_up,
        owned_down,
        owned_bup,
        owned_bdown,
        owned_gone,
        owned_sone,
        owned_gtwo,
        owned_stwo,
    )


def solution(mesh):
    placed = (
        P(("rep", "shard"), None, None),
        P(("rep", "shard"), None),
        P("shard", None),
        P("shard", None),
        P("shard", None),
        P("shard", None),
        P("shard", None),
        P("shard", None),
        P("shard"),
        P("shard"),
        P("shard"),
        P("shard"),
        P("shard"),
        P("shard"),
        P(("rep", "shard"), None, None),
    )
    return jax.shard_map(
        on_device,
        mesh=mesh,
        in_specs=placed,
        out_specs=(
            P(("rep", "shard"), None, None),
            P(("rep", "shard"), None, None),
            P("shard", None),
            P("shard", None),
            P("shard", None),
            P("shard", None),
            P("shard", None),
            P("shard", None),
            P("shard"),
            P("shard"),
            P("shard"),
            P("shard"),
            P("shard"),
            P("shard"),
        ),
        check_vma=False,
    )
```

profile of v0, /device:TPU:0, one launch (start us, length us, event | category | flops | bytes accessed | tf_op | source)
XLA Modules:
  0.0 649.6 jit_solution(12599371499878112364)
XLA Ops:
  9.5 25.0 %all_gather.47 = bf16[512,512]{1,0:T(8,128)(2,1)S(1)} all-gather(bf16[32,512]{1,0:T(8,128)(2,1)} %param.17), channel_id=1, replica_groups=mesh['rep'=2,'shard'=16] {'shard'}, dimensions={0}, use_global_device_ids=true | all-gather | bytes 557056 | tf_op jit(solution)/shard_map/all_gather | solution.py:120
  38.4 30.0 %all-reduce.12 = (bf16[512]{0:T(512)(128)(2,1)S(1)}, bf16[512]{0:T(512)(128)(2,1)S(1)}, bf16[512]{0:T(512)(128)(2,1)S(1)}, bf16[512]{0:T(512)(128)(2,1)S(1)}) all-reduce(bf16[512]{0:T(512)(128)(2,1)S(1)} %dynamic-update-slice.1, bf16[512]{0:T(512)(128)(2,1)S(1)} %dynamic-update-slice, ...), channel_id=1, replica_groups=mesh['rep'=2,'shard'=16] {'shard'}, use_global_device_ids=true, to_apply=%add.1 | all-reduce | flops 2048 | bytes 8192
  72.8 19.4 %all_gather.48 = bf16[512,512]{1,0:T(8,128)(2,1)S(1)} all-gather(bf16[32,512]{1,0:T(8,128)(2,1)S(1)} %copy-done.30), channel_id=1, replica_groups=mesh['rep'=2,'shard'=16] {'shard'}, dimensions={0}, use_global_device_ids=true | all-gather | bytes 557056 | tf_op jit(solution)/shard_map/all_gather | solution.py:121
  95.3 21.1 %all_gather.46 = bf16[512,512]{1,0:T(8,128)(2,1)S(1)} all-gather(bf16[32,512]{1,0:T(8,128)(2,1)S(1)} %copy-done.31), channel_id=1, replica_groups=mesh['rep'=2,'shard'=16] {'shard'}, dimensions={0}, use_global_device_ids=true | all-gather | bytes 557056 | tf_op jit(solution)/shard_map/all_gather | solution.py:122
  117.4 17.9 %all-gather = bf16[16,1,128]{2,1,0:T(2,128)(2,1)S(1)} all-gather(bf16[1,1,128]{2,1,0:T(2,128)(2,1)S(1)} %bitcast.208), channel_id=1, replica_groups=mesh['rep'=2,'shard'=16] {'shard'}, dimensions={0}, use_global_device_ids=true | all-gather | bytes 4352 | tf_op jit(solution)/shard_map/all_gather | solution.py:146
  137.8 4.4 select_reduce_fusion
  145.5 3.8 fusion.93
  149.4 3.8 fusion.94
  153.9 20.3 %all_gather.49 = bf16[512,512]{1,0:T(8,128)(2,1)S(1)} all-gather(bf16[32,512]{1,0:T(8,128)(2,1)S(1)} %copy-done.32), channel_id=1, replica_groups=mesh['rep'=2,'shard'=16] {'shard'}, dimensions={0}, use_global_device_ids=true | all-gather | bytes 557056 | tf_op jit(solution)/shard_map/all_gather | solution.py:123
  175.3 9.5 %multiply_convert_fusion = (bf16[1024,2048]{1,0:T(8,128)(2,1)}, f32[1024,2048]{1,0:T(8,128)}) fusion(f32[2048]{0:T(1024)S(1)} %bitcast.206, bf16[512,2048]{1,0:T(8,128)(2,1)} %all-gather.4.cloned.1.call-done, f32[1024,512]{0,1:T(8,128)S(1)} %get-tuple-element.146, f32[512]{0:T(512)S(1)} %convert_element_type.223, f32[512]{0:T(512)S(1)} %convert_element_type.222, ...), kind=kOutput, calls=%fused_computation.15 | convolution fusion | flops 2171076608 | bytes 16797696 | tf_op jit(solution)/shard_map/dot_general | solution.py:158
  184.8 10.3 %fusion.96 = (bf16[2048]{0:T(1024)(128)(2,1)S(1)}, bf16[1024,2048]{1,0:T(8,128)(2,1)S(1)}) fusion(f32[1024,2048]{1,0:T(8,128)} %get-tuple-element.148, f32[2048]{0:T(1024)S(1)} %bitcast.207, bf16[2048,512]{1,0:T(8,128)(2,1)} %all-gather.6.cloned.1.call-done, bf16[1,1024,512]{2,1,0:T(8,128)(2,1)} %param.29), kind=kOutput, calls=%fused_computation.152 | convolution fusion | flops 2193618944 | bytes 15740928 | tf_op jit(solution)/shard_map/td,fd->tf/dot_general | solution.py:181
  195.1 3.7 fusion.97
  235.5 6.7 %fusion.15 = f32[8,64,1024]{2,1,0:T(8,128)} fusion(bf16[8,512,1024]{2,1,0:T(8,128)(2,1)} %copy-done.45, pred[512,1024]{1,0:T(8,128)(4,1)} %copy-done.25, bf16[1,1024,8,64]{1,3,2,0:T(8,128)(2,1)} %copy-done.11), kind=kOutput, calls=%fused_computation.31 | convolution fusion | flops 541065216 | bytes 11534336 | tf_op jit(solution)/shard_map/while/body/eval_jaxpr/hqk,qhd->khd/dot_general | solution.py:94
  242.2 6.1 add_convert_fusion.2
  253.8 6.6 %convolution_convert_fusion.1 = bf16[512,2048]{1,0:T(8,128)(2,1)} fusion(bf16[1024,2048]{1,0:T(8,128)(2,1)} %copy-done.46, f32[1024,512]{0,1:T(8,128)} %copy-done, f32[512]{0:T(512)S(1)} %convert_element_type.223, f32[512]{0:T(512)S(1)} %convert_element_type.222, f32[1024]{0:T(1024)S(1)} %add_rsqrt_fusion, f32[1024]{0:T(1024)S(1)} %broadcast_multiply_fusion.4), kind=kOutput, calls=%fused_computation.30 | convolution fusion | flops 2151153664 | bytes 8400896 | tf_op jit(solution)/shard_map/td,tf->df/dot_general | solution.py:184
  260.5 6.3 convolution_convert_fusion
  276.3 58.0 %all-reduce.11 = (bf16[512]{0:T(512)(128)(2,1)S(1)}, bf16[2048]{0:T(1024)(128)(2,1)S(1)}, bf16[512]{0:T(512)(128)(2,1)S(1)}, bf16[512]{0:T(512)(128)(2,1)S(1)}, ...) all-reduce(bf16[512]{0:T(512)(128)(2,1)S(1)} %dynamic-update-slice., ...), channel_id=1, replica_groups=mesh['rep'=2,'shard'=16] {'shard'}, use_global_device_ids=true, to_apply=%add.4 | all-reduce | flops 5120 | bytes 20480
  334.3 6.8 %fusion.57 = bf16[1,1024,512]{1,2,0:T(8,128)(2,1)} fusion(f32[1024,512]{0,1:T(8,128)} %copy-done, bf16[1024,2048]{1,0:T(8,128)(2,1)} %get-tuple-element.147, bf16[2048,512]{1,0:T(8,128)(2,1)} %all-gather.6.cloned.1.call-done, f32[512]{0:T(512)S(1)} %convert_element_type.227), kind=kOutput, calls=%fused_computation.99 | convolution fusion | flops 2149056512 | bytes 9439232 | tf_op jit(solution)/shard_map/dot_general | solution.py:165
  346.9 53.4 %reduce-scatter.11.cloned.1.call-done = bf16[32,512]{1,0:T(8,128)(2,1)} async-done(((bf16[512,512]{1,0:T(8,128)(2,1)}), bf16[32,512]{1,0:T(8,128)(2,1)}) %reduce-scatter.11.cloned.1.call-update) | async-done | bytes 32784 | tf_op jit(solution)/shard_map/reduce_scatter | solution.py:241
  400.3 58.6 %reduce-scatter.13.cloned.1.call-done = bf16[32,512]{1,0:T(8,128)(2,1)} async-done(((bf16[512,512]{1,0:T(8,128)(2,1)}), bf16[32,512]{1,0:T(8,128)(2,1)}) %reduce-scatter.13.cloned.1.call-update) | async-done | bytes 32784 | tf_op jit(solution)/shard_map/reduce_scatter | solution.py:244
  459.0 64.2 %reduce-scatter.15.cloned.1.call-done = bf16[32,2048]{1,0:T(8,128)(2,1)} async-done(((bf16[512,2048]{1,0:T(8,128)(2,1)}), bf16[32,2048]{1,0:T(8,128)(2,1)}) %reduce-scatter.15.cloned.1.call-update) | async-done | bytes 131088 | tf_op jit(solution)/shard_map/reduce_scatter | solution.py:247
  523.2 64.8 %reduce-scatter.17.cloned.1.call-done = bf16[128,512]{1,0:T(8,128)(2,1)} async-done(((bf16[2048,512]{1,0:T(8,128)(2,1)}), bf16[128,512]{1,0:T(8,128)(2,1)}) %reduce-scatter.17.cloned.1.call-update) | async-done | bytes 131088 | tf_op jit(solution)/shard_map/reduce_scatter | solution.py:250
  594.5 19.2 %all-reduce.18.cloned.1.call-done = (bf16[32,512]{1,0:T(8,128)(2,1)}, bf16[32,512]{1,0:T(8,128)(2,1)}, bf16[32,512]{1,0:T(8,128)(2,1)}, bf16[32,512]{1,0:T(8,128...) async-done(((bf16[32,512]{1,0:T(8,128)(2,1)}, ...) | async-done | bytes 131664 | tf_op jit(solution)/shard_map/psum | solution.py:300
  626.1 13.2 %all-reduce.20.cloned.1.call-done = (bf16[32,2048]{1,0:T(8,128)(2,1)}, bf16[128,512]{1,0:T(8,128)(2,1)}) async-done(((bf16[32,2048]{1,0:T(8,128)(2,1)}, bf16[128,512]{1,0:T(8,128)(2,1)}), (bf16[32,2048]{1,0:T(8,128)(2,1)}, bf16[128,512]{1,0:T(8,128)(2,1)})) %all-reduce.20.cloned.1.call-update) | async-done | bytes 262160 | tf_op jit(solution)/shard_map/psum | solution.py:304
  (203 shorter events, 99.5 us)
Async XLA Ops:
  7.2 29.0 %copy-start.34 = (u32[32]{0:T(128)S(1)}, u32[32]{0:T(128)}, u32[]{:S(2)}) copy-start(u32[32]{0:T(128)} %constant.91) | copy-start | bytes 388
  7.2 30.2 %copy-start.37 = (bf16[32]{0:T(256)(128)(2,1)S(1)}, bf16[32]{0:T(256)(128)(2,1)}, u32[]{:S(2)}) copy-start(bf16[32]{0:T(256)(128)(2,1)} %param.26) | copy-start | bytes 196
  7.2 30.5 %copy-start.38 = (bf16[32]{0:T(256)(128)(2,1)S(1)}, bf16[32]{0:T(256)(128)(2,1)}, u32[]{:S(2)}) copy-start(bf16[32]{0:T(256)(128)(2,1)} %param.25) | copy-start | bytes 196
  7.2 30.7 %copy-start.39 = (bf16[32]{0:T(256)(128)(2,1)S(1)}, bf16[32]{0:T(256)(128)(2,1)}, u32[]{:S(2)}) copy-start(bf16[32]{0:T(256)(128)(2,1)} %param.28) | copy-start | bytes 196
  7.2 31.0 %copy-start.40 = (bf16[32]{0:T(256)(128)(2,1)S(1)}, bf16[32]{0:T(256)(128)(2,1)}, u32[]{:S(2)}) copy-start(bf16[32]{0:T(256)(128)(2,1)} %param.27) | copy-start | bytes 196
  7.2 168.1 %all-gather.4.cloned.1.call-start = ((), (), s32[]{:S(2)}) async-start(), calls=%async_computation.6 | async-start | bytes 2228224 | tf_op jit(solution)/shard_map/all_gather | solution.py:144
  8.0 176.8 %all-gather.6.cloned.1.call-start = ((), (), s32[]{:S(2)}) async-start(), calls=%async_computation.7 | async-start | bytes 2228224 | tf_op jit(solution)/shard_map/all_gather | solution.py:145
  8.7 338.2 %reduce-scatter.7.cloned.1.call-start = ((), (), s32[]{:S(2)}) async-start(), calls=%async_computation.8 | async-start | bytes 557056 | tf_op jit(solution)/shard_map/reduce_scatter | solution.py:235
  34.5 34.5 %copy-start.13 = (bf16[512,512]{1,0:T(8,128)(2,1)}, bf16[512,512]{1,0:T(8,128)(2,1)S(1)}, u32[]{:S(2)}) copy-start(bf16[512,512]{1,0:T(8,128)(2,1)S(1)} %all_gather.47) | copy-start | bytes 1572868
  116.4 18.8 %copy-start.10 = (bf16[1,1024,512]{2,1,0:T(8,128)(2,1)S(1)}, bf16[1,1024,512]{2,1,0:T(8,128)(2,1)}, u32[]{:S(2)}) copy-start(bf16[1,1024,512]{2,1,0:T(8,128)(2,1)} %param.29) | copy-start | bytes 3145732
  117.3 32.0 %copy-start.5 = (bf16[1024,512]{0,1:T(8,128)(2,1)}, bf16[1024,512]{0,1:T(8,128)(2,1)S(1)}, u32[]{:S(2)}) copy-start(bf16[1024,512]{0,1:T(8,128)(2,1)S(1)} %convolution_convert_fusion.3) | copy-start | bytes 3145732
  117.3 19.2 %copy-start.33 = (s32[1,1024]{1,0:T(1,128)S(1)}, s32[1,1024]{1,0:T(1,128)}, u32[]{:S(2)}) copy-start(s32[1,1024]{1,0:T(1,128)} %param.16) | copy-start | bytes 12292
  137.8 11.6 %copy-start.25 = (pred[512,1024]{1,0:T(8,128)(4,1)}, pred[512,1024]{1,0:T(8,128)(4,1)S(1)}, u32[]{:S(2)}) copy-start(pred[512,1024]{1,0:T(8,128)(4,1)S(1)} %get-tuple-element.127) | copy-start | bytes 1572868
  153.9 21.1 %copy-start.2 = (bf16[1024,8,64]{0,2,1:T(8,128)(2,1)}, bf16[1024,8,64]{0,2,1:T(8,128)(2,1)S(1)}, u32[]{:S(2)}) copy-start(bf16[1024,8,64]{0,2,1:T(8,128)(2,1)S(1)} %pad_maximum_fusion.1) | copy-start | bytes 3145732
  175.0 26.8 %copy-start = (f32[1024,512]{0,1:T(8,128)}, f32[1024,512]{0,1:T(8,128)S(1)}, u32[]{:S(2)}) copy-start(f32[1024,512]{0,1:T(8,128)S(1)} %get-tuple-element.146) | copy-start | bytes 6291460
  184.8 10.3 %copy-start.36 = (bf16[512,2048]{1,0:T(8,128)(2,1)S(1)}, bf16[512,2048]{1,0:T(8,128)(2,1)}, u32[]{:S(2)}) copy-start(bf16[512,2048]{1,0:T(8,128)(2,1)} %all-gather.4.cloned.1.call-done) | copy-start | bytes 6291460
  207.4 9.0 %copy-start.11 = (bf16[1,1024,8,64]{1,3,2,0:T(8,128)(2,1)}, bf16[1,1024,8,64]{1,3,2,0:T(8,128)(2,1)S(1)}, u32[]{:S(2)}) copy-start(bf16[1,1024,8,64]{1,3,2,0:T(8,128)(2,1)S(1)} %get-tuple-element.151) | copy-start | bytes 3145732
  229.6 117.3 %reduce-scatter.9.cloned.1.call-start = ((), (), s32[]{:S(2)}) async-start(), calls=%async_computation.9 | async-start | bytes 557056 | tf_op jit(solution)/shard_map/reduce_scatter | solution.py:238
  242.2 158.1 %reduce-scatter.11.cloned.1.call-start = ((), (), s32[]{:S(2)}) async-start(), calls=%async_computation.10 | async-start | bytes 557056 | tf_op jit(solution)/shard_map/reduce_scatter | solution.py:241
  250.9 208.0 %reduce-scatter.13.cloned.1.call-start = ((), (), s32[]{:S(2)}) async-start(), calls=%async_computation.11 | async-start | bytes 557056 | tf_op jit(solution)/shard_map/reduce_scatter | solution.py:244
  253.7 269.5 %reduce-scatter.15.cloned.1.call-start = ((), (), s32[]{:S(2)}) async-start(), calls=%async_computation.12 | async-start | bytes 2228224 | tf_op jit(solution)/shard_map/reduce_scatter | solution.py:247
  260.5 327.6 %reduce-scatter.17.cloned.1.call-start = ((), (), s32[]{:S(2)}) async-start(), calls=%async_computation.13 | async-start | bytes 2228224 | tf_op jit(solution)/shard_map/reduce_scatter | solution.py:250
  266.8 346.9 %all-reduce.18.cloned.1.call-start = ((), (), s32[]{:S(2)}) async-start(), calls=%async_computation.14 | async-start | bytes 268288 | tf_op jit(solution)/shard_map/psum | solution.py:300
  458.9 180.4 %all-reduce.20.cloned.1.call-start = ((), (), s32[]{:S(2)}) async-start(), calls=%async_computation.15 | async-start | bytes 524288 | tf_op jit(solution)/shard_map/psum | solution.py:304
  (33 other events, 78.3 us)
Sparse Core Ops, SparseCore 0:
  10.2 44.5 all-gather.3
  57.0 41.5 all-gather.5
  229.7 53.5 reduce-scatter.6
  287.1 54.8 reduce-scatter.8
  345.4 54.8 reduce-scatter.10
  404.1 54.7 reduce-scatter.12
  462.6 60.5 reduce-scatter.14
  527.4 60.5 reduce-scatter.16
  591.5 22.1 all-reduce.17
  615.9 23.3 all-reduce.19
where the time goes:
time: 656 us; the launch traced here: 650 us
  waiting for transfers between devices  275 us (42%)
  blocking collectives  192 us (29%)
  matrix products  108 us (16%)
  other arithmetic  31.7 us (5%)
  local copies, waits for them, and re-layouts  25.6 us (4%)
  between operations  17 us (3%)
    unnamed x2, blocking collectives  88 us
    reduce_scatter x1, waiting for transfers between devices, on_device(): lax.psum_scatter(grad_down.astype(jnp.bfloat16), 'shard', scatter_dimensi...  64.8 us
    reduce_scatter x1, waiting for transfers between devices, on_device(): lax.psum_scatter(grad_up.astype(jnp.bfloat16), 'shard', scatter_dimension...  64.2 us
    reduce_scatter x1, waiting for transfers between devices, on_device(): lax.psum_scatter(grad_out.astype(jnp.bfloat16), 'shard', scatter_dimensio...  58.6 us
    reduce_scatter x1, waiting for transfers between devices, on_device(): lax.psum_scatter(grad_value_w.astype(jnp.bfloat16), 'shard', scatter_dime...  53.4 us
    all_gather x1, blocking collectives, on_device(): lax.all_gather(w_query, 'shard', axis=0, tiled=True)  25 us
    all_gather x1, blocking collectives, on_device(): lax.all_gather(w_value, 'shard', axis=0, tiled=True)  21.1 us
    unnamed x115, local copies, waits for them, and re-layouts  20.8 us
  transfers between devices with their start and end apart: 10, of which 6 were waited for; matrix products, arithmetic and copies ran while one was open for 18% of the time, Pallas kernels for 0%

commit v1 on v0

v1 whole, which is shorter than its diff:
```python
import functools
import types

import jax
import jax.numpy as jnp
from jax import lax
from jax.experimental import pallas as pl
from jax.experimental.pallas import tpu as pltpu
from jax.sharding import PartitionSpec as P

WIDTH = 512
CHUNK = 256
HEAD_DIM = 64
GROUP = 256
PER_GROUP = GROUP // HEAD_DIM
GROUPS = WIDTH // GROUP

epsilon = 1e-05
MESH = pl.DeviceIdType.MESH
F32 = jnp.float32
BF16 = jnp.bfloat16


class Place:
    def __init__(self, reps, shards):
        self.reps, self.shards = reps, shards
        self.A = 4
        self.B = shards // 8
        self.r = lax.axis_index("rep")
        s = lax.axis_index("shard")
        self.s = s
        self.c = lax.rem(s, 2)
        self.b = lax.rem(s // 2, self.B)
        self.a = s // (2 * self.B)
        self.h = lax.rem(self.r, 2)

    def at(self, a=None, b=None, c=None, r=None):
        a = self.a if a is None else a
        b = self.b if b is None else b
        c = self.c if c is None else c
        r = self.r if r is None else r
        return (r, (a * self.B + b) * 2 + c)

    def next_a(self, j):
        return lax.rem(self.a + j, self.A)

    def next_b(self, j):
        return lax.rem(self.b + j, self.B)

    def sibling(self):
        return self.at(c=1 - self.c)

    def twin(self, bit=1):
        return self.at(r=self.r + bit - 2 * bit * lax.rem(self.r // bit, 2))

    def bits(self):
        bit, out = 2, []
        while bit < self.reps:
            out.append(bit)
            bit *= 2
        return out

    def partners(self):
        out = [self.sibling(), self.twin()]
        out += [self.at(a=self.next_a(j)) for j in range(1, self.A)]
        out += [self.at(b=self.next_b(j)) for j in range(1, self.B)]
        return out + [self.twin(bit) for bit in self.bits()]


def greet(partners):
    barrier = pltpu.get_barrier_semaphore()
    for device in partners:
        pl.semaphore_signal(barrier, inc=1, device_id=device, device_id_type=MESH)
    pl.semaphore_wait(barrier, len(partners))


def remote(src, dst, send, recv, device):
    return pltpu.make_async_remote_copy(
        src_ref=src, dst_ref=dst, send_sem=send, recv_sem=recv, device_id=device, device_id_type=MESH
    )


def both(one, two):
    if one is None:
        return two
    return one if two is None else jnp.logical_and(one, two)


class Sends:
    def __init__(self):
        self.made = []

    @staticmethod
    def act(copy, do):
        cond, make = copy()
        if cond is None:
            do(make())
        else:
            pl.when(cond)(lambda: do(make()))

    def go(self, copy):
        self.act(copy, lambda made: made.start())
        self.made.append(copy)

    def arrived(self, copy):
        self.act(copy, lambda made: made.wait_recv())

    def finish(self):
        for copy in self.made:
            self.act(copy, lambda made: made.wait_send())
        self.made = []


class Gather:
    def __init__(self, place, full, lo, rows, send, recv, sends):
        self.p, self.full, self.lo, self.rows = place, full, lo, rows
        self.send, self.recv, self.sends = send, recv, sends

    def whole(self, a, b, c):
        return self.full.at[a, b, c, pl.ds(self.lo, self.rows)]

    def half(self, a, b, c, h):
        size = self.rows // 2
        return self.full.at[a, b, c, pl.ds(pl.multiple_of(self.lo + h * size, 16), size)]

    def line(self, k, way):
        p = self.p
        if k == 0:
            return None, p.a
        return ((p.a - k >= 0), p.a - k) if way > 0 else ((p.a + k < p.A), p.a + k)

    def cross(self, j, way):
        p = self.p
        if j == 0:
            return None, p.b
        return ((p.b - j >= 0), p.b - j) if way > 0 else ((p.b + j < p.B), p.b + j)

    def copy(self, ref, a, b, c, kind, half_id, device):
        return remote(ref, ref, self.send.at[a, b, kind], self.recv.at[a, b, c, half_id], device)

    def to_a(self, k, way, step):
        p = self.p

        def copy():
            cond, a = self.line(k, way)
            cond = both(cond, (p.a < p.A - 1) if step > 0 else (p.a > 0))
            ref = self.whole(a, p.b, p.c)
            return cond, lambda: self.copy(
                ref, a, p.b, p.c, 1 if step > 0 else 0, 0, p.at(a=p.a + step)
            )

        self.sends.go(copy)

    def to_b(self, k, way, j, across, step):
        p = self.p

        def copy():
            cond, a = self.line(k, way)
            more, b = self.cross(j, across)
            cond = both(both(cond, more), (p.b < p.B - 1) if step > 0 else (p.b > 0))
            ref = self.half(a, b, p.c, p.h)
            return cond, lambda: self.copy(
                ref, a, b, p.c, 3 if step > 0 else 2, 0, p.at(b=p.b + step)
            )

        self.sends.go(copy)

    def column(self, k, way):
        p = self.p
        for step in (1, -1):
            if k == 0 or step == way:
                self.to_a(k, way, step)
        for step in (1, -1):
            self.to_b(k, way, 0, 0, step)

        def copy():
            cond, a = self.line(k, way)
            return cond, lambda: self.copy(
                self.whole(a, p.b, p.c), a, p.b, p.c, 5, 0, p.sibling()
            )

        self.sends.go(copy)

    def own(self):
        self.column(0, 1)

    def ways(self, k):
        return (1,) if k == 0 else (1, -1)

    def columns(self, k):
        p = self.p
        for way in self.ways(k):

            def copy():
                cond, a = self.line(k, way)
                return cond, lambda: self.copy(
                    self.whole(a, p.b, p.c), a, p.b, p.c, 0, 0, p.sibling()
                )

            self.sends.arrived(copy)
            self.column(k, way)

    def rows_b(self, k):
        p = self.p
        for way in self.ways(k):
            for j in range(1, p.B):
                for across in (1, -1):

                    def copy(kind, half_id, device, way=way, j=j, across=across):
                        cond, a = self.line(k, way)
                        more, b = self.cross(j, across)
                        ref = self.half(a, b, p.c, p.h)
                        return both(cond, more), lambda: self.copy(
                            ref, a, b, p.c, kind, half_id, device()
                        )

                    self.sends.arrived(functools.partial(copy, 0, 0, p.sibling))
                    if p.B > 2:
                        self.to_b(k, way, j, across, across)
                    self.sends.go(functools.partial(copy, 4, 1, p.twin))
                    self.sends.go(functools.partial(copy, 5, 0, p.sibling))

    def rows_twin(self, k):
        p = self.p
        for way in self.ways(k):
            for j in range(1, p.B):

                def copy(kind, way=way, j=j):
                    cond, a = self.line(k, way)
                    b = p.next_b(j)
                    ref = self.half(a, b, p.c, 1 - p.h)
                    return cond, lambda: self.copy(ref, a, b, p.c, kind, 1, p.sibling())

                self.sends.arrived(functools.partial(copy, 0))
                self.sends.go(functools.partial(copy, 6))

    def rest(self):
        p = self.p
        other = 1 - p.c
        for a in range(p.A):
            self.copy(self.whole(a, p.b, other), a, p.b, other, 0, 0, p.sibling()).wait_recv()
            for j in range(1, p.B):
                b = p.next_b(j)
                for i, h in enumerate((p.h, 1 - p.h)):
                    self.copy(self.half(a, b, other, h), a, b, other, 0, i, p.sibling()).wait_recv()


class SmallGather:
    def __init__(self, place, full, send, recv, sends):
        self.p, self.full, self.send, self.recv, self.sends = place, full, send, recv, sends

    def copy(self, ref, k, device):
        return remote(ref, ref, self.send.at[k], self.recv.at[k], device)

    def own(self):
        p = self.p
        for j in range(1, p.A):
            self.sends.go(
                lambda j=j: (
                    None,
                    lambda: self.copy(self.full.at[p.a, p.b, p.c], j, p.at(a=p.next_a(j))),
                )
            )

    def second(self):
        p = self.p
        for j in range(1, p.A):
            self.copy(self.full.at[p.next_a(p.A - j), p.b, p.c], j, p.sibling()).wait_recv()
        for j in range(1, p.B):
            self.sends.go(
                lambda j=j: (
                    None,
                    lambda: self.copy(self.full.at[:, p.b, p.c], p.A + j, p.at(b=p.next_b(j))),
                )
            )

    def third(self):
        p = self.p
        for j in range(1, p.B):
            self.copy(self.full.at[:, p.next_b(p.B - j), p.c], p.A + j, p.sibling()).wait_recv()
        self.sends.go(lambda: (None, lambda: self.copy(self.full.at[:, :, p.c], 0, p.sibling())))

    def last(self):
        p = self.p
        self.copy(self.full.at[:, :, 1 - p.c], 0, p.sibling()).wait_recv()


class Reduce:
    def __init__(self, place, part, bufs, lo, rows, at, lanes, send, recv, sends, pair_first=False):
        self.p, self.part, self.lo, self.rows, self.at, self.lanes = place, part, lo, rows, at, lanes
        self.core, self.line_b, self.pair, self.line_a, self.wide, self.done = bufs
        self.send, self.recv, self.sends = send, recv, sends
        self.pair_first = pair_first

    def win(self):
        return (pl.ds(self.lo, self.rows), pl.ds(self.at, self.lanes))

    def half(self, h):
        size = self.lanes // 2
        return (
            pl.ds(self.lo, self.rows),
            pl.ds(pl.multiple_of(self.at + h * size, 128), size),
        )

    def go(self, copy):
        self.sends.go(lambda: (None, lambda: self.copy(*copy())))

    def copy(self, src, dst, k, device):
        return remote(src, dst, self.send.at[k], self.recv.at[k], device)

    def arrived(self, ref, k):
        self.copy(ref, ref, k, self.p.sibling()).wait_recv()

    def order(self):
        return list(range(1, self.p.B)) + [0]

    def start(self):
        p = self.p
        for j in self.order():
            self.go(
                lambda j=j: (
                    self.part.at[(slice(None), p.next_b(j), 1 - p.c) + self.win()],
                    self.core.at[(slice(None), j) + self.win()],
                    j,
                    p.sibling(),
                )
            )

    def after_core(self):
        p = self.p
        for j in self.order():
            mine = (slice(None), p.next_b(j), p.c) + self.win()
            got = (slice(None), j) + self.win()
            self.arrived(self.core.at[got], j)
            self.part[mine] = self.part[mine] + self.core[got]
            if self.pair_first:
                self.to_pair(j)
            elif j > 0:
                self.to_b(j, self.win)

    def to_b(self, j, win):
        p = self.p
        self.go(
            lambda: (
                self.part.at[(slice(None), p.next_b(j), p.c) + win()],
                self.line_b.at[(j - 1, slice(None)) + win()],
                p.B + j,
                p.at(b=p.next_b(j)),
            )
        )

    def to_pair(self, j):
        p = self.p
        self.go(
            lambda: (
                self.part.at[(slice(None), p.next_b(j), p.c) + self.half(1 - p.h)],
                self.pair.at[(slice(None), j) + self.half(1 - p.h)],
                2 * p.B + j,
                p.twin(),
            )
        )

    def to_a(self):
        p = self.p
        for j in range(1, p.A):
            self.go(
                lambda j=j: (
                    self.part.at[(p.next_a(j), p.b, p.c) + self.half(p.h)],
                    self.line_a.at[(j - 1,) + self.half(p.h)],
                    3 * p.B + j,
                    p.at(a=p.next_a(j)),
                )
            )

    def add_b(self, win):
        p = self.p
        mine = (slice(None), p.b, p.c) + win
        total = self.part[mine].astype(F32)
        for j in range(1, p.B):
            got = (j - 1, slice(None)) + win
            self.arrived(self.line_b.at[got], p.B + j)
            total = total + self.line_b[got].astype(F32)
        self.part[mine] = total.astype(BF16)

    def add_pair(self, j):
        p = self.p
        got = (slice(None), j) + self.half(p.h)
        mine = (slice(None), p.next_b(j), p.c) + self.half(p.h)
        self.arrived(self.pair.at[got], 2 * p.B + j)
        self.part[mine] = self.part[mine] + self.pair[got]

    def second(self):
        p = self.p
        if self.pair_first:
            for j in self.order():
                self.add_pair(j)
                if j > 0:
                    self.to_b(j, lambda: self.half(p.h))
        else:
            self.add_b(self.win())
            self.to_pair(0)

    def third(self):
        p = self.p
        if self.pair_first:
            self.add_b(self.half(p.h))
        else:
            self.add_pair(0)
        self.to_a()

    def after_a(self):
        p, base = self.p, 3 * self.p.B
        mine = self.half(p.h)
        total = self.part[(p.a, p.b, p.c) + mine].astype(F32)
        for j in range(1, p.A):
            got = (j - 1,) + mine
            self.arrived(self.line_a.at[got], base + j)
            total = total + self.line_a[got].astype(F32)
        for i, bit in enumerate(p.bits()):
            k = base + p.A + 1 + i
            self.wide[(2 * i,) + mine] = total.astype(BF16)

            def copy(i=i, k=k, bit=bit):
                here = self.half(p.h)
                return (
                    self.wide.at[(2 * i,) + here],
                    self.wide.at[(2 * i + 1,) + here],
                    k,
                    p.twin(bit),
                )

            self.go(copy)
            self.arrived(self.wide.at[(2 * i + 1,) + mine], k)
            total = self.wide[(2 * i,) + mine].astype(F32)
            total = total + self.wide[(2 * i + 1,) + mine].astype(F32)
        self.done[mine] = total.astype(BF16)
        self.go(
            lambda: (
                self.done.at[self.half(p.h)],
                self.done.at[self.half(p.h)],
                base + p.A,
                p.twin(),
            )
        )

    def finish(self):
        p = self.p
        self.arrived(self.done.at[self.half(1 - p.h)], 3 * p.B + p.A)

    def steps(self):
        return [self.start, self.after_core, self.second, self.third, self.after_a, self.finish]

    @staticmethod
    def n_sems(reps, shards):
        return 3 * (shards // 8) + 4 + 1 + max(reps.bit_length() - 2, 0)


class SmallReduce:
    def __init__(self, place, slots, send, recv, sends):
        self.p, self.slots, self.send, self.recv, self.sends = place, slots, send, recv, sends
        self.now, self.free, self.k = 0, 1, 0

    def copy(self, src, dst, k, device):
        return remote(self.slots.at[src], self.slots.at[dst], self.send.at[k], self.recv.at[k], device)

    def exchange(self, devices):
        self.fresh = []
        for device in devices:
            src, dst, k = self.now, self.free, self.k
            self.fresh.append((dst, k))
            self.sends.go(
                lambda src=src, dst=dst, k=k, device=device: (
                    None,
                    lambda: self.copy(src, dst, k, device()),
                )
            )
            self.free, self.k = self.free + 1, self.k + 1

    def add(self):
        total = self.slots[self.now]
        for slot, k in self.fresh:
            self.copy(slot, slot, k, self.p.sibling()).wait_recv()
            total = total + self.slots[slot]
        self.slots[self.free] = total
        self.now, self.free = self.free, self.free + 1

    def steps(self):
        p = self.p
        stages = [
            [p.sibling],
            [lambda j=j: p.at(b=p.next_b(j)) for j in range(1, p.B)],
            [p.twin],
            [lambda j=j: p.at(a=p.next_a(j)) for j in range(1, p.A)],
        ] + [[functools.partial(p.twin, bit)] for bit in p.bits()]
        out = [lambda: self.exchange(stages[0])]
        for stage in stages[1:]:
            out.append(lambda stage=stage: (self.add(), self.exchange(stage)))
        out.append(self.add)
        return out

    @staticmethod
    def counts(reps, shards):
        wide = max(reps.bit_length() - 2, 0)
        copies = 1 + (shards // 8 - 1) + 1 + 3 + wide
        return copies, 1 + copies + 4 + wide


def dot(lhs, rhs):
    return lax.dot_general(lhs, rhs, (((1,), (0,)), ((), ())), preferred_element_type=F32)


def dot_nt(lhs, rhs):
    return lax.dot_general(lhs, rhs, (((1,), (1,)), ((), ())), preferred_element_type=F32)


def dot_tn(lhs, rhs):
    return lax.dot_general(lhs, rhs, (((0,), (0,)), ((), ())), preferred_element_type=F32)


def iota(shape, axis):
    return lax.broadcasted_iota(jnp.int32, shape, axis)


def mean_last(value):
    return jnp.sum(value, axis=-1, keepdims=True) * (1.0 / value.shape[-1])


def column_sum(value):
    return jnp.sum(value, axis=0, keepdims=True)


def twice(value):
    return jnp.concatenate([value, value], axis=1)


def feature(value):
    return jnp.where(value > 0, value + 1.0, jnp.exp(jnp.minimum(value, 0.0)))


def layer_kernel(reps, shards, length, n):
    p = Place(reps, shards)
    A, B = p.A, p.B
    rows_w = n.w_query.shape[0]
    R = rows_w
    chunks = length // CHUNK
    full, part, smalls, slots, vecs = n.full, n.part, n.smalls, n.slots, n.vecs

    mine = full.at[p.a, p.b, p.c]
    pieces = [
        (ref, mine.at[pl.ds(i * R, R)])
        for i, ref in enumerate((n.w_query, n.w_key, n.w_value, n.w_out))
    ]
    pieces += [
        (n.w_up.at[:, pl.ds(i * WIDTH, WIDTH)], mine.at[pl.ds((4 + i) * R, R)]) for i in range(4)
    ]
    pieces += [(n.w_down, mine.at[pl.ds(8 * R, 4 * R)])]
    local = [
        pltpu.make_async_copy(src, dst, n.sem_local.at[i]) for i, (src, dst) in enumerate(pieces)
    ]
    for copy in local:
        copy.start()
    smalls[p.a, p.b, p.c] = n.small[...]
    greet(p.partners())
    for copy in local:
        copy.wait()

    sends = Sends()
    tiny = SmallGather(p, smalls, n.send0, n.recv0, sends)
    first = Gather(p, full, 0, 4 * R, n.send1.at[0], n.recv1.at[0], sends)
    later = Gather(p, full, 4 * R, 8 * R, n.send1.at[1], n.recv1.at[1], sends)
    bufs = (n.core, n.line_b, n.pair, n.line_a, n.wide, n.done)

    def job(i, lo, rows, at, lanes, pair_first=False):
        return Reduce(
            p, part, bufs, lo, rows, at, lanes, n.send2.at[i], n.recv2.at[i], sends, pair_first
        )

    jobs = [
        job(0, 4 * R, 2 * R, 0, WIDTH),
        job(1, 6 * R, 2 * R, 0, WIDTH),
        job(2, 8 * R, 4 * R, 0, WIDTH, True),
        job(3, 3 * R, R, 0, WIDTH),
        job(4, 0, 3 * R, 0, GROUP),
        job(5, 0, 3 * R, GROUP, GROUP),
    ]
    J = [j.steps() for j in jobs]
    small_sum = SmallReduce(p, slots, n.send3, n.recv3, sends)
    T = small_sum.steps()

    def rows_of(t):
        return pl.ds(pl.multiple_of(t * CHUNK, CHUNK), CHUNK)

    def per_chunk(events, body, down=False):
        def step(i, carry):
            body(chunks - 1 - i if down else i)
            for at, calls in enumerate(events):
                if calls:

                    @pl.when(i == at)
                    def _():
                        for call in calls:
                            call()

            return carry

        lax.fori_loop(0, chunks, step, 0)

    tiny.own()
    first.own()

    seg_row = n.segment_ids[...].astype(F32)
    seg_rows = n.seg_rows
    seg_rows[0:8, :] = jnp.full((8, 128), -1.0, F32)
    seg_rows[pl.ds(8, length), :] = jnp.broadcast_to(seg_row, (128, length)).T
    seg_rows[pl.ds(8 + length, 8), :] = jnp.full((8, 128), -2.0, F32)
    heads, mask, mask_t = n.heads, n.mask, n.mask_t
    for i in range(PER_GROUP):
        heads[i] = jnp.where(iota((CHUNK, GROUP), 1) // HEAD_DIM == i, 1.0, 0.0).astype(BF16)
    same_head = (iota((GROUP, GROUP), 0) // HEAD_DIM) == (iota((GROUP, GROUP), 1) // HEAD_DIM)
    n.ones[...] = jnp.where(same_head, 1.0, 0.0).astype(BF16)
    later_row = iota((CHUNK, CHUNK), 0) >= iota((CHUNK, CHUNK), 1)
    later_col = iota((CHUNK, CHUNK), 0) <= iota((CHUNK, CHUNK), 1)
    for t in range(chunks):
        same = twice(seg_rows[pl.ds(8 + t * CHUNK, CHUNK), :]) == seg_row[
            :, t * CHUNK : (t + 1) * CHUNK
        ]
        mask[t] = jnp.where(same & later_row, 1.0, 0.0).astype(BF16)
        mask_t[t] = jnp.where(same & later_col, 1.0, 0.0).astype(BF16)

    def seg_chunk(t):
        return seg_rows[pl.ds(pl.multiple_of(8 + t * CHUNK, 8), CHUNK), :]

    def seg_at(t, row):
        return seg_rows[pl.ds(8 + t * CHUNK + row, 1), :]

    def flags(one, two):
        return twice(jnp.where(one == two, 1.0, 0.0))

    first.columns(1)
    tiny.second()
    first.rows_b(0)

    def norm_one(t):
        at = rows_of(t)
        h = n.inputs[at].astype(F32)
        centre = h - mean_last(h)
        scale = lax.rsqrt(mean_last(centre * centre) + epsilon)
        n.normal_one[at] = centre * scale
        n.scale_one[at] = jnp.broadcast_to(scale, (CHUNK, 128))

    per_chunk([], norm_one)
    first.columns(2)
    first.rows_b(1)
    first.rows_twin(0)
    tiny.third()
    first.columns(3)
    first.rows_b(2)
    first.rows_twin(1)
    later.own()
    first.rows_b(3)
    first.rows_twin(2)
    tiny.last()

    blocks = smalls[...].reshape(shards * 8, 128).astype(BF16)
    lane = iota((128, WIDTH), 1)
    row = iota((128, WIDTH), 0)
    block = iota((shards, 8, WIDTH), 0)
    at_lane = iota((shards, 8, WIDTH), 2)
    spread = jnp.where(lane % R == row, 1.0, 0.0).astype(BF16)
    laid = dot(blocks, spread).reshape(shards, 8, WIDTH)
    vecs[0:8] = jnp.sum(jnp.where(at_lane // R == block, laid, 0.0), axis=0)
    spread = jnp.where(lane % (4 * R) == row, 1.0, 0.0).astype(BF16)
    laid = dot(blocks, spread).reshape(shards, 8, WIDTH)
    for i in range(4):
        picked = jnp.where((at_lane + i * WIDTH) // (4 * R) == block, laid, 0.0)
        vecs[8 + i : 9 + i] = jnp.sum(picked, axis=0)[0:1]
    b_down, gain_one, shift_one, gain_two, shift_two = (vecs[i : i + 1] for i in range(1, 6))

    first.rows_twin(3)
    first.rest()

    def weight(i):
        return full[:, :, :, i * R : (i + 1) * R, :].reshape(WIDTH, WIDTH)

    def weight_down(i):
        return full[i, :, :, 8 * R : 12 * R, :].reshape(WIDTH, WIDTH)

    lanes = [slice(g * GROUP, (g + 1) * GROUP) for g in range(GROUPS)]
    state, state_now, keys_now = n.state, n.state_now, n.keys_now
    state_now[...] = jnp.zeros(state_now.shape, F32)
    keys_now[...] = jnp.zeros(keys_now.shape, F32)
    slots[0] = jnp.zeros(slots.shape[1:], F32)

    def forward(t):
        at = rows_of(t)
        normed = (n.normal_one[at] * gain_one + shift_one).astype(BF16)
        n.normed_attn[at] = normed
        n.query[at] = feature(dot(normed, weight(0))).astype(BF16)
        n.key[at] = feature(dot(normed, weight(1))).astype(BF16)
        n.value[at] = dot(normed, weight(2)).astype(BF16)
        seg = seg_chunk(t)
        before = flags(seg, seg_at(t, -1))
        ending = flags(seg, seg_at(t, CHUNK - 1)).astype(BF16)
        carry = flags(seg_at(t, CHUNK - 1), seg_at(t, -1))
        before_low = before.astype(BF16)
        for g in range(GROUPS):
            q, k, v = (ref[at, lanes[g]] for ref in (n.query, n.key, n.value))
            old = state_now[g].astype(BF16)
            state[g, t] = old
            mixed = dot(q * before_low, old)
            for i in range(PER_GROUP):
                scores = dot_nt(q * heads[i], k).astype(BF16) * mask[t]
                mixed = mixed + dot(scores, v * heads[i])
            sums = dot(mask[t], k) + before * keys_now[g, 0:1]
            n.key_sums[at, lanes[g]] = sums
            totals = dot((q.astype(F32) * sums).astype(BF16), n.ones[...])
            inverse = 1.0 / totals
            n.inverse[at, lanes[g]] = inverse
            n.context[at, lanes[g]] = (mixed * inverse).astype(BF16)
            ended = k * ending
            state_now[g] = state_now[g] * carry + dot_tn(ended, v) * n.ones[...].astype(F32)
            keys_now[g, 0:1] = keys_now[g, 0:1] * carry + column_sum(ended.astype(F32))
        after = n.inputs[at].astype(F32) + dot(n.context[at], weight(3))
        centre = after - mean_last(after)
        scale = lax.rsqrt(mean_last(centre * centre) + epsilon)
        normal = centre * scale
        n.normal_two[at] = normal
        n.scale_two[at] = jnp.broadcast_to(scale, (CHUNK, 128))
        n.normed_ffn[at] = (normal * gain_two + shift_two).astype(BF16)
        n.result[at] = after + b_down

    per_chunk(
        [
            [lambda: later.columns(1), lambda: later.rows_b(0)],
            [lambda: later.columns(2), lambda: later.rows_b(1), lambda: later.rows_twin(0)],
            [lambda: later.columns(3), lambda: later.rows_b(2), lambda: later.rows_twin(1)],
            [lambda: later.rows_b(3), lambda: later.rows_twin(2)],
        ],
        forward,
    )
    later.rows_twin(3)
    later.rest()

    c0 = 0.7978845608028654
    c1 = c0 * 0.044715
    n.grad_normed[...] = jnp.zeros(n.grad_normed.shape, F32)

    def ffn(i, events):
        bias = vecs[8 + i : 9 + i]

        def body(t):
            at = rows_of(t)
            pre = dot(n.normed_ffn[at], weight(4 + i)) + bias
            square = pre * pre
            half = 0.5 + 0.5 * jnp.tanh(pre * (c0 + c1 * square))
            hidden = pre * half
            slope = half + (2.0 * hidden) * (1.0 - half) * (c0 + (3.0 * c1) * square)
            low = hidden.astype(BF16)
            n.hidden[at] = low
            n.result[at] = n.result[at] + dot(low, weight_down(i))
            grad = (dot_nt(n.cotangent[at], weight_down(i)) * slope).astype(BF16)
            n.grad_pre[at] = grad
            slots[0, i : i + 1] += column_sum(grad.astype(F32))
            n.grad_normed[at] = n.grad_normed[at] + dot_nt(grad, weight(4 + i))

        per_chunk(events, body)
        for m in range(2):
            cut = slice(m * 256, (m + 1) * 256)
            grad = dot_tn(n.hidden[:, cut], n.cotangent[...]).astype(BF16)
            part[i, m * B // 2 : (m + 1) * B // 2, :, 8 * R : 12 * R, :] = grad.reshape(
                B // 2, 2, 4 * R, WIDTH
            )
            grad = dot_tn(n.normed_ffn[:, cut], n.grad_pre[...]).astype(BF16)
            part[2 * m : 2 * m + 2, :, :, (4 + i) * R : (5 + i) * R, :] = grad.reshape(
                2, B, 2, R, WIDTH
            )

    ffn(0, [])
    ffn(1, [])
    J[0][0]()
    ffn(2, [[], [], [J[0][1]], []])
    ffn(3, [[], [], [J[0][2]], []])
    J[1][0]()
    J[2][0]()
    J[0][3]()

    def norm_two_back(t):
        at = rows_of(t)
        n.output[at] = n.result[at].astype(BF16)
        grad = n.grad_normed[at]
        normal = n.normal_two[at]
        up = n.cotangent[at].astype(F32)
        slots[0, 4:5] += column_sum(up)
        slots[0, 7:8] += column_sum(grad * normal)
        slots[0, 8:9] += column_sum(grad)
        e = grad * gain_two
        back = e - mean_last(e) - normal * mean_last(e * normal)
        after = up + n.scale_two[at][:, 0:1] * back
        n.grad_normed[at] = after
        low = after.astype(BF16)
        n.grad_attn[at] = low
        grad_context = dot_nt(low, weight(3)).astype(BF16).astype(F32)
        inverse = n.inverse[at]
        n.grad_mixed[at] = (grad_context * inverse).astype(BF16)
        turned = (grad_context * n.context[at].astype(F32)).astype(BF16)
        for g in range(GROUPS):
            n.grad_totals[at, lanes[g]] = -dot(turned[:, lanes[g]], n.ones[...]) * inverse[
                :, lanes[g]
            ]

    per_chunk([[], [J[1][1], J[2][1]], [], []], norm_two_back)
    for m in range(2):
        grad = dot_tn(n.context[:, m * 256 : (m + 1) * 256], n.grad_attn[...]).astype(BF16)
        part[2 * m : 2 * m + 2, :, :, 3 * R : 4 * R, :] = grad.reshape(2, B, 2, R, WIDTH)
    J[3][0]()
    J[0][4]()

    def backward(g):
        state_now[g] = jnp.zeros((GROUP, GROUP), F32)
        keys_now[g] = jnp.zeros((8, GROUP), F32)

        def body(t):
            at = rows_of(t)
            seg = seg_chunk(t)
            before = flags(seg, seg_at(t, -1)).astype(BF16)
            after = flags(seg, seg_at(t, CHUNK))
            opening = flags(seg, seg_at(t, 0)).astype(BF16)
            carry = flags(seg_at(t, 0), seg_at(t, CHUNK))
            q, k, v, gm = (
                ref[at, lanes[g]] for ref in (n.query, n.key, n.value, n.grad_mixed)
            )
            totals = n.grad_totals[at, lanes[g]]
            old = state_now[g].astype(BF16)
            weighted = totals * q.astype(F32)
            gq = dot_nt(gm * before, state[g, t]) + totals * n.key_sums[at, lanes[g]]
            gk = after * (dot_nt(v, old) + keys_now[g, 0:1]) + dot(mask_t[t], weighted.astype(BF16))
            gv = after * dot(k, old)
            for i in range(PER_GROUP):
                head = heads[i]
                gm_head = gm * head
                back = dot_nt(gm_head, v).astype(BF16) * mask[t]
                gq = gq + dot(back, k * head)
                back = dot_nt(v * head, gm).astype(BF16) * mask_t[t]
                gk = gk + dot(back, q * head)
                back = dot_nt(k * head, q).astype(BF16) * mask_t[t]
                gv = gv + dot(back, gm_head)
            n.grad_query[at, lanes[g]] = (gq * jnp.minimum(q.astype(F32), 1.0)).astype(BF16)
            n.grad_key[at, lanes[g]] = (gk * jnp.minimum(k.astype(F32), 1.0)).astype(BF16)
            n.grad_value[at, lanes[g]] = gv.astype(BF16)
            opened = q * opening
            state_now[g] = state_now[g] * carry + dot_tn(opened, gm) * n.ones[...].astype(F32)
            keys_now[g, 0:1] = keys_now[g, 0:1] * carry + column_sum(
                weighted * opening.astype(F32)
            )

        return body

    def weight_grads(g):
        for i, ref in enumerate((n.grad_query, n.grad_key, n.grad_value)):
            grad = dot_tn(n.normed_attn[...], ref[:, lanes[g]]).astype(BF16)
            part[:, :, :, i * R : (i + 1) * R, lanes[g]] = grad.reshape(A, B, 2, R, GROUP)

    per_chunk([[J[0][5], J[1][2], J[2][2]], [], [J[3][1]], []], backward(0), down=True)
    weight_grads(0)
    J[4][0]()
    J[1][3]()
    J[2][3]()
    per_chunk([[J[4][1], J[3][2]], [J[1][4]], [J[2][4], J[3][3]], [J[4][2]]], backward(1), down=True)
    weight_grads(1)
    J[5][0]()
    J[1][5]()
    J[3][4]()

    def norm_one_back(t):
        at = rows_of(t)
        grad = dot_nt(n.grad_query[at], weight(0))
        grad = grad + dot_nt(n.grad_key[at], weight(1))
        grad = grad + dot_nt(n.grad_value[at], weight(2))
        normal = n.normal_one[at]
        slots[0, 5:6] += column_sum(grad * normal)
        slots[0, 6:7] += column_sum(grad)
        e = grad * gain_one
        back = e - mean_last(e) - normal * mean_last(e * normal)
        n.grad_inputs[at] = n.grad_normed[at] + n.scale_one[at][:, 0:1] * back

    per_chunk([[J[2][5], J[4][3]], [J[5][1]], [J[3][5]], []], norm_one_back)
    T[0]()
    J[4][4]()
    T[1]()
    J[5][2]()
    T[2]()
    J[4][5]()
    J[5][3]()
    T[3]()
    J[5][4]()
    for step in T[4:]:
        step()

    total = slots[small_sum.now]
    high = total.astype(BF16)
    low = (total - high.astype(F32)).astype(BF16)
    row, lane = iota((WIDTH, 128), 0), iota((WIDTH, 128), 1)
    pick = jnp.where((row == lane + p.s * R) & (lane < R), 1.0, 0.0).astype(BF16)
    n.tiny_out[0:16] = dot(high, pick) + dot(low, pick)
    picked = jnp.zeros((16, 128), F32)
    for i in range(4):
        wanted = (row + i * WIDTH == lane + p.s * (4 * R)) & (lane < 4 * R)
        pick = jnp.where(wanted, 1.0, 0.0).astype(BF16)
        keep = iota((16, 128), 0) == i
        picked = picked + jnp.where(keep, dot(high, pick) + dot(low, pick), 0.0)
    n.tiny_out[16:17] = column_sum(picked)

    J[5][5]()
    done = n.done
    for i, ref in enumerate((n.out_query, n.out_key, n.out_value, n.out_out)):
        ref[...] = done[i * R : (i + 1) * R].astype(F32)
    for i in range(4):
        n.out_up[:, i * WIDTH : (i + 1) * WIDTH] = done[(4 + i) * R : (5 + i) * R].astype(F32)
    n.out_down[...] = done[8 * R : 12 * R].astype(F32)
    sends.finish()


def layer(reps, shards, inputs, segment_ids, weights, small, cotangent):
    length = inputs.shape[0]
    A, B = 4, shards // 8
    R = weights[0].shape[0]
    rows = 12 * R
    bits = max(reps.bit_length() - 2, 0)
    copies, n_slots = SmallReduce.counts(reps, shards)
    n_sems = Reduce.n_sems(reps, shards)
    w_query, w_key, w_value, w_out, w_up, w_down = weights
    ins = dict(
        inputs=inputs,
        segment_ids=segment_ids,
        w_query=w_query,
        w_key=w_key,
        w_value=w_value,
        w_out=w_out,
        w_up=w_up,
        w_down=w_down,
        small=small,
        cotangent=cotangent,
    )
    outs = dict(
        output=((length, WIDTH), BF16),
        grad_inputs=((length, WIDTH), F32),
        out_query=((R, WIDTH), F32),
        out_key=((R, WIDTH), F32),
        out_value=((R, WIDTH), F32),
        out_out=((R, WIDTH), F32),
        out_up=((R, 4 * WIDTH), F32),
        out_down=((4 * R, WIDTH), F32),
        tiny_out=((24, 128), F32),
    )
    tall = (length, WIDTH)
    buffers = dict(
        full=((A, B, 2, rows, WIDTH), BF16),
        part=((A, B, 2, rows, WIDTH), BF16),
        core=((A, B, rows, WIDTH), BF16),
        line_b=((B - 1, A, rows, WIDTH), BF16),
        pair=((A, B, rows, WIDTH), BF16),
        line_a=((A - 1, rows, WIDTH), BF16),
        wide=((max(2 * bits, 1), rows if bits else 16, WIDTH), BF16),
        done=((rows, WIDTH), BF16),
        smalls=((A, B, 2, 8, 128), F32),
        slots=((n_slots, 16, WIDTH), F32),
        vecs=((16, WIDTH), F32),
        seg_rows=((length + 16, 128), F32),
        heads=((PER_GROUP, CHUNK, GROUP), BF16),
        ones=((GROUP, GROUP), BF16),
        mask=((length // CHUNK, CHUNK, CHUNK), BF16),
        mask_t=((length // CHUNK, CHUNK, CHUNK), BF16),
        normal_one=(tall, F32),
        scale_one=((length, 128), F32),
        normed_attn=(tall, BF16),
        query=(tall, BF16),
        key=(tall, BF16),
        value=(tall, BF16),
        key_sums=(tall, F32),
        inverse=(tall, F32),
        context=(tall, BF16),
        state=((GROUPS, length // CHUNK, GROUP, GROUP), BF16),
        state_now=((GROUPS, GROUP, GROUP), F32),
        keys_now=((GROUPS, 8, GROUP), F32),
        normal_two=(tall, F32),
        scale_two=((length, 128), F32),
        normed_ffn=(tall, BF16),
        hidden=(tall, BF16),
        grad_pre=(tall, BF16),
        grad_normed=(tall, F32),
        grad_attn=(tall, BF16),
        grad_mixed=(tall, BF16),
        grad_totals=(tall, F32),
    )
    sems = dict(
        sem_local=(9,),
        send0=(A + B,),
        recv0=(A + B,),
        send1=(2, A, B, 7),
        recv1=(2, A, B, 2, 2),
        send2=(6, n_sems),
        recv2=(6, n_sems),
        send3=(copies,),
        recv3=(copies,),
    )
    names = list(ins) + list(outs) + list(buffers) + list(sems)

    def kernel(*refs):
        n = types.SimpleNamespace(**dict(zip(names, refs, strict=True)))
        n.result = n.grad_inputs
        n.grad_query, n.grad_key, n.grad_value = n.hidden, n.grad_pre, n.normed_ffn
        layer_kernel(reps, shards, length, n)

    vmem = pl.BlockSpec(memory_space=pltpu.VMEM)
    flops = 2 * 3 * length * WIDTH * WIDTH * 12 + 20 * length * length * WIDTH
    results = pl.pallas_call(
        kernel,
        out_shape=tuple(jax.ShapeDtypeStruct(*spec) for spec in outs.values()),
        in_specs=[vmem] * len(ins),
        out_specs=(vmem,) * len(outs),
        scratch_shapes=[pltpu.VMEM(*spec) for spec in buffers.values()]
        + [pltpu.SemaphoreType.DMA(shape) for shape in sems.values()],
        compiler_params=pltpu.CompilerParams(
            collective_id=1, has_side_effects=True, vmem_limit_bytes=63 << 20
        ),
        cost_estimate=pl.CostEstimate(flops=flops, bytes_accessed=8 << 20, transcendentals=0),
        name="layer",
    )(*ins.values())
    return dict(zip(outs, results, strict=True))


def on_device(
    reps,
    shards,
    inputs,
    segment_ids,
    w_query,
    w_key,
    w_value,
    w_out,
    w_up,
    w_down,
    b_up,
    b_down,
    gain_attn,
    shift_attn,
    gain_ffn,
    shift_ffn,
    cotangent,
):
    sequences, length, width = inputs.shape
    R = w_query.shape[0]

    def padded(vec):
        return jnp.pad(vec.astype(F32), (0, 128 - vec.shape[0]))[None]

    small = jnp.concatenate(
        [padded(v) for v in (b_up, b_down, gain_attn, shift_attn, gain_ffn, shift_ffn)]
        + [jnp.zeros((2, 128), F32)],
        axis=0,
    )
    got = layer(
        reps,
        shards,
        inputs.reshape(sequences * length, width),
        segment_ids,
        (w_query, w_key, w_value, w_out, w_up, w_down),
        small,
        cotangent.reshape(sequences * length, width),
    )
    tiny = got["tiny_out"]
    return (
        got["output"].reshape(inputs.shape),
        got["grad_inputs"].reshape(inputs.shape),
        got["out_query"],
        got["out_key"],
        got["out_value"],
        got["out_out"],
        got["out_up"],
        got["out_down"],
        tiny[16, : 4 * R],
        *(tiny[i, :R] for i in range(4, 9)),
    )


def solution(mesh):
    reps, shards = mesh.shape["rep"], mesh.shape["shard"]
    token = P(("rep", "shard"), None, None)
    matrix, vector = P("shard", None), P("shard")
    return jax.shard_map(
        functools.partial(on_device, reps, shards),
        mesh=mesh,
        in_specs=(token, P(("rep", "shard"), None)) + (matrix,) * 6 + (vector,) * 6 + (token,),
        out_specs=(token, token) + (matrix,) * 6 + (vector,) * 6,
        check_vma=False,
    )
```

time: 656 us -> 147 us (0.22)
  waiting for transfers between devices: 275 us -> 0 us
  blocking collectives: 192 us -> 0 us
  Pallas kernels: 0 us -> 133 us
  matrix products: 108 us -> 0 us
  other arithmetic: 31.7 us -> 2.03 us
  between operations: 17 us -> 0.7 us
  local copies, waits for them, and re-layouts: 25.6 us -> 10.7 us
    reduce_scatter x6 -> x0, waiting for transfers between devices: 241 us -> none  [the longest x1 64.8 us: on_device(): lax.psum_scatter(grad_down.astype(jnp.bfloat16), 'shard', scatter_dimensi...]
    pallas_call x0 -> x1, Pallas kernels: none -> 133 us  [layer(): pl.pallas_call(kernel, out_shape=tuple((jax.ShapeDtypeStruct(*spec) for s...]
    dot_general x30 -> x0, matrix products: 108 us -> none  [the longest x2 12.8 us: attend_backward(): jnp.einsum('hqk,qhd->khd', rounded, mixed_block, preferred_element_type=j...]
    all_gather x5 -> x0, blocking collectives: 104 us -> none  [the longest x1 25 us: on_device(): lax.all_gather(w_query, 'shard', axis=0, tiled=True)]
    unnamed x2 -> x0, blocking collectives: 88 us -> none
    psum x2 -> x0, waiting for transfers between devices: 32.4 us -> none  [the longest x1 19.2 us: on_device(): lax.psum(part_q.astype(jnp.bfloat16), 'rep').astype(jnp.float32)]
    convert_element_type x20 -> x0, other arithmetic: 19.2 us -> none  [the longest x1 2.87 us: on_device(): key_pull(grad_kfeat.reshape(row_count, model_width))[0].astype(jnp.bfloat16)]
    unnamed x115 -> x22, local copies, waits for them, and re-layouts: 20.8 us -> 7.53 us
  transfers between devices with their start and end apart: 10 -> 0, of which waited for: 6 -> 0; matrix products, arithmetic and copies ran while one was open for 18% -> 0% of each run, Pallas kernels for 0% -> 0%
where the time goes in v1:
time: 147 us; the launch traced here: 146 us
  Pallas kernels  133 us (90%)
  local copies, waits for them, and re-layouts  10.7 us (7%)
  other arithmetic  2.03 us (1%)
    pallas_call x1, Pallas kernels, layer(): pl.pallas_call(kernel, out_shape=tuple((jax.ShapeDtypeStruct(*spec) for s...  133 us
    unnamed x22, local copies, waits for them, and re-layouts  7.53 us

profile of v1, /device:TPU:0, one launch (start us, length us, event | category | flops | bytes accessed | tf_op | source)
XLA Modules:
  0.0 146.4 jit_solution(419483131215513667)
XLA Ops:
  0.6 0.7 bitcast_convert_fusion
  1.3 0.7 bitcast_convert_fusion.2
  2.0 0.7 bitcast_convert_fusion.4
  2.7 0.6 concatenate.3.refs_8_
  3.3 132.9 %layer.1 = (bf16[1024,512]{1,0:T(8,128)(2,1)}, f32[1024,512]{1,0:T(8,128)}, f32[32,512]{1,0:T(8,128)}, f32[32,512]{1,0:T(8,128)}, f32[32,512]{1,0:T(8,128)}, /*i...) custom-call(bf16[1024,512]{1,0:T(8,128)(2,1)} %bitcast.36, s32[1,1024]{1,0:T(1,128)} %refs_1_.1, ...), custom_call_target="tpu_custom_call" | custom-call | flops 30064771072 | bytes 8388608 | tf_op jit(solution)/shard_map/layer/pallas_call | solution.py:1016
  136.2 0.0 copy-start
  136.2 1.4 slice_bitcast_fusion
  137.6 1.2 slice_bitcast_fusion.5
  138.8 2.3 %copy.37 = bf16[1,1024,512]{2,1,0:T(8,128)(2,1)} copy(bf16[1,1024,512]{2,1,0:T(8,128)(2,1)} %bitcast.35) | data formatting | bytes 2097152
  141.1 0.0 copy-done
  141.1 0.0 copy-start.3
  141.1 0.0 copy-start.2
  141.1 0.0 copy-start.1
  141.1 1.3 copy.38
  142.4 0.0 copy-done.6
  142.4 0.6 copy.39
  143.1 0.0 copy-done.5
  143.1 0.6 copy.40
  143.7 0.0 copy-done.4
  143.7 0.6 copy.41
  144.3 0.0 copy-done.3
  144.3 0.6 copy.42
  145.0 0.7 copy.43
  145.7 0.7 copy.44
  (6 shorter events, 0.0 us)
Async XLA Ops:
  136.2 4.8 %copy-start = (f32[1024,512]{1,0:T(8,128)S(1)}, f32[1024,512]{1,0:T(8,128)}, u32[]{:S(2)}) copy-start(f32[1024,512]{1,0:T(8,128)} %get-tuple-element.24) | copy-start | bytes 6291460
  141.1 1.4 copy-start.6
  141.1 2.0 %copy-start.5 = (f32[32,512]{1,0:T(8,128)S(1)}, f32[32,512]{1,0:T(8,128)}, u32[]{:S(2)}) copy-start(f32[32,512]{1,0:T(8,128)} %get-tuple-element.60) | copy-start | bytes 196612
  141.1 2.6 %copy-start.4 = (f32[32,512]{1,0:T(8,128)S(1)}, f32[32,512]{1,0:T(8,128)}, u32[]{:S(2)}) copy-start(f32[32,512]{1,0:T(8,128)} %get-tuple-element.61) | copy-start | bytes 196612
  141.1 3.3 %copy-start.3 = (f32[32,512]{1,0:T(8,128)S(1)}, f32[32,512]{1,0:T(8,128)}, u32[]{:S(2)}) copy-start(f32[32,512]{1,0:T(8,128)} %get-tuple-element.62) | copy-start | bytes 196612
  141.1 3.9 %copy-start.2 = (f32[32,2048]{1,0:T(8,128)S(1)}, f32[32,2048]{1,0:T(8,128)}, u32[]{:S(2)}) copy-start(f32[32,2048]{1,0:T(8,128)} %get-tuple-element.63) | copy-start | bytes 786436
  141.1 4.6 %copy-start.1 = (f32[128,512]{1,0:T(8,128)S(1)}, f32[128,512]{1,0:T(8,128)}, u32[]{:S(2)}) copy-start(f32[128,512]{1,0:T(8,128)} %get-tuple-element.64) | copy-start | bytes 786436

commit v2 on v1

--- a/solution.py
+++ b/solution.py
@@ -41,6 +41,10 @@
         r = self.r if r is None else r
         return (r, (a * self.B + b) * 2 + c)
 
+    def near(self, k):
+        high = self.a // 2
+        return (1 - self.a + 4 * high, 2 - high, 3 * (1 - high))[k]
+
     def next_a(self, j):
         return lax.rem(self.a + j, self.A)
 
@@ -112,137 +116,120 @@
 
 
 class Gather:
-    def __init__(self, place, full, lo, rows, send, recv, sends):
-        self.p, self.full, self.lo, self.rows = place, full, lo, rows
-        self.send, self.recv, self.sends = send, recv, sends
+    def __init__(self, place, full, window, send, recv, base, sends):
+        self.p, self.full = place, full
+        self.lo, self.rows, self.left, self.lanes = window
+        self.send, self.recv, self.base, self.sends = send, recv, base, sends
 
     def whole(self, a, b, c):
-        return self.full.at[a, b, c, pl.ds(self.lo, self.rows)]
+        return self.full.at[a, b, c, pl.ds(self.lo, self.rows), pl.ds(self.left, self.lanes)]
 
     def half(self, a, b, c, h):
-        size = self.rows // 2
-        return self.full.at[a, b, c, pl.ds(pl.multiple_of(self.lo + h * size, 16), size)]
-
-    def line(self, k, way):
-        p = self.p
-        if k == 0:
-            return None, p.a
-        return ((p.a - k >= 0), p.a - k) if way > 0 else ((p.a + k < p.A), p.a + k)
-
-    def cross(self, j, way):
-        p = self.p
-        if j == 0:
-            return None, p.b
-        return ((p.b - j >= 0), p.b - j) if way > 0 else ((p.b + j < p.B), p.b + j)
-
-    def copy(self, ref, a, b, c, kind, half_id, device):
-        return remote(ref, ref, self.send.at[a, b, kind], self.recv.at[a, b, c, half_id], device)
-
-    def to_a(self, k, way, step):
-        p = self.p
-
-        def copy():
-            cond, a = self.line(k, way)
-            cond = both(cond, (p.a < p.A - 1) if step > 0 else (p.a > 0))
-            ref = self.whole(a, p.b, p.c)
-            return cond, lambda: self.copy(
-                ref, a, p.b, p.c, 1 if step > 0 else 0, 0, p.at(a=p.a + step)
-            )
-
-        self.sends.go(copy)
-
-    def to_b(self, k, way, j, across, step):
-        p = self.p
-
-        def copy():
-            cond, a = self.line(k, way)
-            more, b = self.cross(j, across)
-            cond = both(both(cond, more), (p.b < p.B - 1) if step > 0 else (p.b > 0))
-            ref = self.half(a, b, p.c, p.h)
-            return cond, lambda: self.copy(
-                ref, a, b, p.c, 3 if step > 0 else 2, 0, p.at(b=p.b + step)
-            )
-
-        self.sends.go(copy)
-
-    def column(self, k, way):
-        p = self.p
-        for step in (1, -1):
-            if k == 0 or step == way:
-                self.to_a(k, way, step)
-        for step in (1, -1):
-            self.to_b(k, way, 0, 0, step)
-
-        def copy():
-            cond, a = self.line(k, way)
-            return cond, lambda: self.copy(
-                self.whole(a, p.b, p.c), a, p.b, p.c, 5, 0, p.sibling()
-            )
-
-        self.sends.go(copy)
+        size = self.lanes // 2
+        lanes = pl.ds(pl.multiple_of(self.left + h * size, 128), size)
+        return self.full.at[a, b, c, pl.ds(self.lo, self.rows), lanes]
+
+    def copy(self, ref, k, device, other=None):
+        return remote(ref, ref, self.send.at[k], self.recv.at[k if other is None else other], device)
+
+    def go(self, make):
+        self.sends.go(lambda: (None, make))
+
+    def slot(self, kind, k=0, j=0):
+        more = self.p.B - 1
+        j = max(j - 1, 0)
+        base = (0, 4, 4 + more, 4 + 4 * more, 7 + 4 * more, 7 + 7 * more)
+        base += (8 + 7 * more, 8 + 8 * more, 11 + 8 * more)
+        return self.base + base[kind] + (k * more if kind in (2, 4) else k) + j
 
     def own(self):
-        self.column(0, 1)
-
-    def ways(self, k):
-        return (1,) if k == 0 else (1, -1)
-
-    def columns(self, k):
-        p = self.p
-        for way in self.ways(k):
-
-            def copy():
-                cond, a = self.line(k, way)
-                return cond, lambda: self.copy(
-                    self.whole(a, p.b, p.c), a, p.b, p.c, 0, 0, p.sibling()
+        p = self.p
+        for k in (2, 1, 0):
+            self.go(
+                lambda k=k: self.copy(
+                    self.half(p.a, p.b, p.c, p.h) if k else self.whole(p.a, p.b, p.c),
+                    self.slot(0, k),
+                    p.at(a=p.near(k)),
+                    self.slot(0, p.a),
                 )
-
-            self.sends.arrived(copy)
-            self.column(k, way)
-
-    def rows_b(self, k):
-        p = self.p
-        for way in self.ways(k):
-            for j in range(1, p.B):
-                for across in (1, -1):
-
-                    def copy(kind, half_id, device, way=way, j=j, across=across):
-                        cond, a = self.line(k, way)
-                        more, b = self.cross(j, across)
-                        ref = self.half(a, b, p.c, p.h)
-                        return both(cond, more), lambda: self.copy(
-                            ref, a, b, p.c, kind, half_id, device()
-                        )
-
-                    self.sends.arrived(functools.partial(copy, 0, 0, p.sibling))
-                    if p.B > 2:
-                        self.to_b(k, way, j, across, across)
-                    self.sends.go(functools.partial(copy, 4, 1, p.twin))
-                    self.sends.go(functools.partial(copy, 5, 0, p.sibling))
-
-    def rows_twin(self, k):
-        p = self.p
-        for way in self.ways(k):
-            for j in range(1, p.B):
-
-                def copy(kind, way=way, j=j):
-                    cond, a = self.line(k, way)
-                    b = p.next_b(j)
-                    ref = self.half(a, b, p.c, 1 - p.h)
-                    return cond, lambda: self.copy(ref, a, b, p.c, kind, 1, p.sibling())
-
-                self.sends.arrived(functools.partial(copy, 0))
-                self.sends.go(functools.partial(copy, 6))
+            )
+        for j in range(1, p.B):
+            self.go(
+                lambda j=j: self.copy(
+                    self.whole(p.a, p.b, p.c), self.slot(1, 0, j), p.at(b=p.next_b(j))
+                )
+            )
+        self.go(lambda: self.copy(self.whole(p.a, p.b, p.c), self.slot(5), p.sibling()))
+
+    def line_a(self, k):
+        p = self.p
+        place = (p.near(k), p.b, p.c)
+        ref = self.half(*place, p.h) if k else self.whole(*place)
+        self.copy(ref, self.slot(0, p.near(k)), p.sibling()).wait_recv()
+
+        def mine():
+            return self.half(p.near(k), p.b, p.c, p.h)
+
+        for j in range(1, p.B):
+            self.go(lambda j=j: self.copy(mine(), self.slot(2, k, j), p.at(b=p.next_b(j))))
+        if k:
+            self.go(lambda: self.copy(mine(), self.slot(3, k), p.twin()))
+
+    def line_b_own(self):
+        p = self.p
+        for j in range(1, p.B):
+            b = p.next_b(p.B - j)
+            self.copy(self.whole(p.a, b, p.c), self.slot(1, 0, j), p.sibling()).wait_recv()
+            self.go(
+                lambda j=j: self.copy(
+                    self.whole(p.a, p.next_b(p.B - j), p.c), self.slot(6, 0, j), p.sibling()
+                )
+            )
+
+    def line_b(self, k):
+        p = self.p
+        for j in range(1, p.B):
+            b = p.next_b(p.B - j)
+            ref = self.half(p.near(k), b, p.c, p.h)
+            self.copy(ref, self.slot(2, k, j), p.sibling()).wait_recv()
+            self.go(
+                lambda j=j: self.copy(
+                    self.half(p.near(k), p.next_b(p.B - j), p.c, p.h), self.slot(4, k, j), p.twin()
+                )
+            )
+        self.go(
+            lambda: self.copy(
+                self.half(p.near(k), slice(None), p.c, p.h), self.slot(7, k), p.sibling()
+            )
+        )
+
+    def twin(self, k):
+        p = self.p
+        for j in range(0 if k else 1, p.B):
+            ref = self.half(p.near(k), p.next_b(p.B - j), p.c, 1 - p.h)
+            kind = 4 if j else 3
+            self.copy(ref, self.slot(kind, k, j), p.sibling()).wait_recv()
+        self.go(
+            lambda: self.copy(
+                self.half(p.near(k), slice(None), p.c, 1 - p.h), self.slot(8, k), p.sibling()
+            )
+        )
 
     def rest(self):
         p = self.p
         other = 1 - p.c
-        for a in range(p.A):
-            self.copy(self.whole(a, p.b, other), a, p.b, other, 0, 0, p.sibling()).wait_recv()
-            for j in range(1, p.B):
-                b = p.next_b(j)
-                for i, h in enumerate((p.h, 1 - p.h)):
-                    self.copy(self.half(a, b, other, h), a, b, other, 0, i, p.sibling()).wait_recv()
+        self.copy(self.whole(p.a, p.b, other), self.slot(5), p.sibling()).wait_recv()
+        for j in range(1, p.B):
+            ref = self.whole(p.a, p.next_b(p.B - j), other)
+            self.copy(ref, self.slot(6, 0, j), p.sibling()).wait_recv()
+        for k in range(3):
+            for kind, h in ((7, p.h), (8, 1 - p.h)):
+                ref = self.half(p.near(k), slice(None), other, h)
+                self.copy(ref, self.slot(kind, k), p.sibling()).wait_recv()
+
+    @staticmethod
+    def n_sems(shards):
+        return 14 + 8 * (shards // 8 - 1)
 
 
 class SmallGather:
@@ -286,11 +273,29 @@
 
 
 class Reduce:
-    def __init__(self, place, part, bufs, lo, rows, at, lanes, send, recv, sends, pair_first=False):
-        self.p, self.part, self.lo, self.rows, self.at, self.lanes = place, part, lo, rows, at, lanes
+    def __init__(self, place, part, bufs, window, sems, base, sends, pair_first=False, span=None, end=None):
+        self.p, self.part = place, part
+        self.lo, self.rows, self.at, self.lanes = window
         self.core, self.line_b, self.pair, self.line_a, self.wide, self.done = bufs
-        self.send, self.recv, self.sends = send, recv, sends
+        self.send, self.recv = sems
+        self.sends = sends
         self.pair_first = pair_first
+        self.first, self.last = span or (0, place.A)
+        self.end = end or self
+        self.base = base
+
+    def slot(self, kind, j=0):
+        B = self.p.B
+        twins = B if self.pair_first else 1
+        base = (0, B - 1, 2 * B - 1, 2 * B - 2 + twins, 2 * B + 2 + twins, 2 * B + 3 + twins)
+        return self.base + base[kind] + j
+
+    def n_sems(self):
+        last = self.slot(3, 1) if self.end is not self else self.slot(5, len(self.p.bits()))
+        return last - self.base
+
+    def span(self):
+        return slice(self.first, self.last)
 
     def win(self):
         return (pl.ds(self.lo, self.rows), pl.ds(self.at, self.lanes))
@@ -302,8 +307,8 @@
             pl.ds(pl.multiple_of(self.at + h * size, 128), size),
         )
 
-    def go(self, copy):
-        self.sends.go(lambda: (None, lambda: self.copy(*copy())))
+    def go(self, copy, when=lambda: None):
+        self.sends.go(lambda: (when(), lambda: self.copy(*copy())))
 
     def copy(self, src, dst, k, device):
         return remote(src, dst, self.send.at[k], self.recv.at[k], device)
@@ -319,9 +324,9 @@
         for j in self.order():
             self.go(
                 lambda j=j: (
-                    self.part.at[(slice(None), p.next_b(j), 1 - p.c) + self.win()],
-                    self.core.at[(slice(None), j) + self.win()],
-                    j,
+                    self.part.at[(self.span(), p.next_b(j), 1 - p.c) + self.win()],
+                    self.core.at[(self.span(), j) + self.win()],
+                    self.slot(0, j),
                     p.sibling(),
                 )
             )
@@ -329,9 +334,9 @@
     def after_core(self):
         p = self.p
         for j in self.order():
-            mine = (slice(None), p.next_b(j), p.c) + self.win()
-            got = (slice(None), j) + self.win()
-            self.arrived(self.core.at[got], j)
+            mine = (self.span(), p.next_b(j), p.c) + self.win()
+            got = (self.span(), j) + self.win()
+            self.arrived(self.core.at[got], self.slot(0, j))
             self.part[mine] = self.part[mine] + self.core[got]
             if self.pair_first:
                 self.to_pair(j)
@@ -342,9 +347,9 @@
         p = self.p
         self.go(
             lambda: (
-                self.part.at[(slice(None), p.next_b(j), p.c) + win()],
-                self.line_b.at[(j - 1, slice(None)) + win()],
-                p.B + j,
+                self.part.at[(self.span(), p.next_b(j), p.c) + win()],
+                self.line_b.at[(j - 1, self.span()) + win()],
+                self.slot(1, j),
                 p.at(b=p.next_b(j)),
             )
         )
@@ -353,40 +358,47 @@
         p = self.p
         self.go(
             lambda: (
-                self.part.at[(slice(None), p.next_b(j), p.c) + self.half(1 - p.h)],
-                self.pair.at[(slice(None), j) + self.half(1 - p.h)],
-                2 * p.B + j,
+                self.part.at[(self.span(), p.next_b(j), p.c) + self.half(1 - p.h)],
+                self.pair.at[(self.span(), j) + self.half(1 - p.h)],
+                self.slot(2, j),
                 p.twin(),
             )
         )
 
     def to_a(self):
-        p = self.p
+        p, end = self.p, self.end
+        partial = self.last - self.first < p.A
         for j in range(1, p.A):
-            self.go(
+
+            def when(j=j):
+                a = p.next_a(j)
+                return both(a >= self.first, a < self.last) if partial else None
+
+            end.go(
                 lambda j=j: (
                     self.part.at[(p.next_a(j), p.b, p.c) + self.half(p.h)],
                     self.line_a.at[(j - 1,) + self.half(p.h)],
-                    3 * p.B + j,
+                    end.slot(3, j),
                     p.at(a=p.next_a(j)),
-                )
+                ),
+                when,
             )
 
     def add_b(self, win):
         p = self.p
-        mine = (slice(None), p.b, p.c) + win
+        mine = (self.span(), p.b, p.c) + win
         total = self.part[mine].astype(F32)
         for j in range(1, p.B):
-            got = (j - 1, slice(None)) + win
-            self.arrived(self.line_b.at[got], p.B + j)
+            got = (j - 1, self.span()) + win
+            self.arrived(self.line_b.at[got], self.slot(1, j))
             total = total + self.line_b[got].astype(F32)
         self.part[mine] = total.astype(BF16)
 
     def add_pair(self, j):
         p = self.p
-        got = (slice(None), j) + self.half(p.h)
-        mine = (slice(None), p.next_b(j), p.c) + self.half(p.h)
-        self.arrived(self.pair.at[got], 2 * p.B + j)
+        got = (self.span(), j) + self.half(p.h)
+        mine = (self.span(), p.next_b(j), p.c) + self.half(p.h)
+        self.arrived(self.pair.at[got], self.slot(2, j))
         self.part[mine] = self.part[mine] + self.pair[got]
 
     def second(self):
@@ -409,15 +421,15 @@
         self.to_a()
 
     def after_a(self):
-        p, base = self.p, 3 * self.p.B
+        p = self.p
         mine = self.half(p.h)
         total = self.part[(p.a, p.b, p.c) + mine].astype(F32)
         for j in range(1, p.A):
             got = (j - 1,) + mine
-            self.arrived(self.line_a.at[got], base + j)
+            self.arrived(self.line_a.at[got], self.slot(3, j))
             total = total + self.line_a[got].astype(F32)
         for i, bit in enumerate(p.bits()):
-            k = base + p.A + 1 + i
+            k = self.slot(5, i)
             self.wide[(2 * i,) + mine] = total.astype(BF16)
 
             def copy(i=i, k=k, bit=bit):
@@ -438,21 +450,17 @@
             lambda: (
                 self.done.at[self.half(p.h)],
                 self.done.at[self.half(p.h)],
-                base + p.A,
+                self.slot(4),
                 p.twin(),
             )
         )
 
     def finish(self):
         p = self.p
-        self.arrived(self.done.at[self.half(1 - p.h)], 3 * p.B + p.A)
+        self.arrived(self.done.at[self.half(1 - p.h)], self.slot(4))
 
     def steps(self):
         return [self.start, self.after_core, self.second, self.third, self.after_a, self.finish]
-
-    @staticmethod
-    def n_sems(reps, shards):
-        return 3 * (shards // 8) + 4 + 1 + max(reps.bit_length() - 2, 0)
 
 
 class SmallReduce:
@@ -554,36 +562,47 @@
         (n.w_up.at[:, pl.ds(i * WIDTH, WIDTH)], mine.at[pl.ds((4 + i) * R, R)]) for i in range(4)
     ]
     pieces += [(n.w_down, mine.at[pl.ds(8 * R, 4 * R)])]
+    pieces += [(n.inputs_far, n.inputs), (n.cotangent_far, n.cotangent)]
     local = [
         pltpu.make_async_copy(src, dst, n.sem_local.at[i]) for i, (src, dst) in enumerate(pieces)
     ]
     for copy in local:
         copy.start()
-    smalls[p.a, p.b, p.c] = n.small[...]
+    smalls[p.a, p.b, p.c] = jnp.zeros((8, 128), F32)
+    vectors = (n.b_up, n.b_down, n.gain_attn, n.shift_attn, n.gain_ffn, n.shift_ffn)
+    for i, ref in enumerate(vectors):
+        size = ref.shape[0]
+        smalls[p.a, p.b, p.c, i : i + 1, 0:size] = ref[...].astype(F32).reshape(1, size)
     greet(p.partners())
-    for copy in local:
+    for copy in local[:9]:
         copy.wait()
 
     sends = Sends()
     tiny = SmallGather(p, smalls, n.send0, n.recv0, sends)
-    first = Gather(p, full, 0, 4 * R, n.send1.at[0], n.recv1.at[0], sends)
-    later = Gather(p, full, 4 * R, 8 * R, n.send1.at[1], n.recv1.at[1], sends)
+    windows = ((0 * R, 3 * R, 0, 512), (3 * R, 5 * R, 0, 512), (8 * R, 4 * R, 0, 512))
+    gather_0, gather_1, gather_2 = (
+        Gather(p, full, window, n.send1, n.recv1, i * Gather.n_sems(shards), sends)
+        for i, window in enumerate(windows)
+    )
     bufs = (n.core, n.line_b, n.pair, n.line_a, n.wide, n.done)
 
-    def job(i, lo, rows, at, lanes, pair_first=False):
-        return Reduce(
-            p, part, bufs, lo, rows, at, lanes, n.send2.at[i], n.recv2.at[i], sends, pair_first
-        )
-
-    jobs = [
-        job(0, 4 * R, 2 * R, 0, WIDTH),
-        job(1, 6 * R, 2 * R, 0, WIDTH),
-        job(2, 8 * R, 4 * R, 0, WIDTH, True),
-        job(3, 3 * R, R, 0, WIDTH),
-        job(4, 0, 3 * R, 0, GROUP),
-        job(5, 0, 3 * R, GROUP, GROUP),
-    ]
-    J = [j.steps() for j in jobs]
+    made = []
+
+    def job(lo, rows, at=0, lanes=WIDTH, **more):
+        base = sum(one.n_sems() for one in made)
+        window = (lo * R, rows * R, at, lanes)
+        made.append(Reduce(p, part, bufs, window, (n.send1, n.recv2), base, sends, **more))
+        return made[-1]
+
+    up_one = job(4, 2)
+    up_two = job(6, 2)
+    down_one = job(8, 4, pair_first=True, span=(0, 2))
+    down_two = job(8, 4, pair_first=True, span=(2, 4), end=down_one)
+    out_all = job(3, 1)
+    attn_one = job(0, 3, 0, 256)
+    attn_two = job(0, 1, 256, 256)
+    attn_three = job(1, 2, 256, 256, pair_first=True)
+    assert sum(one.n_sems() for one in made) <= n.recv2.shape[0]
     small_sum = SmallReduce(p, slots, n.send3, n.recv3, sends)
     T = small_sum.steps()
 
@@ -605,8 +624,16 @@
 
         lax.fori_loop(0, chunks, step, 0)
 
-    tiny.own()
-    first.own()
+    gather_0.own()
+    gather_0.line_b_own()
+    gather_1.own()
+    gather_0.line_a(1)
+    gather_0.line_a(2)
+    gather_0.line_a(0)
+    gather_0.line_b(0)
+    gather_0.line_b(2)
+    gather_1.line_b_own()
+    gather_2.own()
 
     seg_row = n.segment_ids[...].astype(F32)
     seg_rows = n.seg_rows
@@ -636,30 +663,35 @@
     def flags(one, two):
         return twice(jnp.where(one == two, 1.0, 0.0))
 
-    first.columns(1)
-    tiny.second()
-    first.rows_b(0)
-
+    tiny.own()
+    gather_0.line_b(1)
+    gather_1.line_a(2)
+
+    local[9].wait()
     def norm_one(t):
         at = rows_of(t)
         h = n.inputs[at].astype(F32)
         centre = h - mean_last(h)
         scale = lax.rsqrt(mean_last(centre * centre) + epsilon)
-        n.normal_one[at] = centre * scale
+        n.normal_one[at] = (centre * scale).astype(BF16)
         n.scale_one[at] = jnp.broadcast_to(scale, (CHUNK, 128))
 
     per_chunk([], norm_one)
-    first.columns(2)
-    first.rows_b(1)
-    first.rows_twin(0)
+    gather_1.line_a(1)
+    tiny.second()
+    gather_0.twin(2)
+    gather_1.line_b(2)
+    gather_1.line_a(0)
+    gather_1.line_b(1)
+    gather_0.twin(0)
+    gather_0.twin(1)
+    gather_0.rest()
     tiny.third()
-    first.columns(3)
-    first.rows_b(2)
-    first.rows_twin(1)
-    later.own()
-    first.rows_b(3)
-    first.rows_twin(2)
     tiny.last()
+    gather_2.line_a(0)
+    gather_2.line_b_own()
+    gather_2.line_a(2)
+    gather_1.line_b(0)
 
     blocks = smalls[...].reshape(shards * 8, 128).astype(BF16)
     lane = iota((128, WIDTH), 1)
@@ -676,8 +708,6 @@
         vecs[8 + i : 9 + i] = jnp.sum(picked, axis=0)[0:1]
     b_down, gain_one, shift_one, gain_two, shift_two = (vecs[i : i + 1] for i in range(1, 6))
 
-    first.rows_twin(3)
-    first.rest()
 
     def weight(i):
         return full[:, :, :, i * R : (i + 1) * R, :].reshape(WIDTH, WIDTH)
@@ -691,104 +721,127 @@
     keys_now[...] = jnp.zeros(keys_now.shape, F32)
     slots[0] = jnp.zeros(slots.shape[1:], F32)
 
-    def forward(t):
-        at = rows_of(t)
-        normed = (n.normal_one[at] * gain_one + shift_one).astype(BF16)
-        n.normed_attn[at] = normed
-        n.query[at] = feature(dot(normed, weight(0))).astype(BF16)
-        n.key[at] = feature(dot(normed, weight(1))).astype(BF16)
-        n.value[at] = dot(normed, weight(2)).astype(BF16)
-        seg = seg_chunk(t)
-        before = flags(seg, seg_at(t, -1))
-        ending = flags(seg, seg_at(t, CHUNK - 1)).astype(BF16)
-        carry = flags(seg_at(t, CHUNK - 1), seg_at(t, -1))
-        before_low = before.astype(BF16)
-        for g in range(GROUPS):
-            q, k, v = (ref[at, lanes[g]] for ref in (n.query, n.key, n.value))
+    def forward(g):
+        cut = lanes[g]
+
+        def weight_part(i):
+            return full[:, :, :, i * R : (i + 1) * R, cut].reshape(WIDTH, GROUP)
+
+        def body(t):
+            at = rows_of(t)
+            if g == 0:
+                normed = (n.normal_one[at].astype(F32) * gain_one + shift_one).astype(BF16)
+                n.normed_attn[at] = normed
+            else:
+                normed = n.normed_attn[at]
+            q = feature(dot(normed, weight_part(0))).astype(BF16)
+            k = feature(dot(normed, weight_part(1))).astype(BF16)
+            v = dot(normed, weight_part(2)).astype(BF16)
+            n.query[at, cut], n.key[at, cut], n.value[at, cut] = q, k, v
+            seg = seg_chunk(t)
+            before = flags(seg, seg_at(t, -1))
+            ending = flags(seg, seg_at(t, CHUNK - 1)).astype(BF16)
+            carry = flags(seg_at(t, CHUNK - 1), seg_at(t, -1))
             old = state_now[g].astype(BF16)
             state[g, t] = old
-            mixed = dot(q * before_low, old)
+            mixed = dot(q * before.astype(BF16), old)
             for i in range(PER_GROUP):
                 scores = dot_nt(q * heads[i], k).astype(BF16) * mask[t]
                 mixed = mixed + dot(scores, v * heads[i])
             sums = dot(mask[t], k) + before * keys_now[g, 0:1]
-            n.key_sums[at, lanes[g]] = sums
+            n.key_sums[at, cut] = sums
             totals = dot((q.astype(F32) * sums).astype(BF16), n.ones[...])
             inverse = 1.0 / totals
-            n.inverse[at, lanes[g]] = inverse
-            n.context[at, lanes[g]] = (mixed * inverse).astype(BF16)
+            n.inverse[at, cut] = inverse
+            n.context[at, cut] = (mixed * inverse).astype(BF16)
             ended = k * ending
             state_now[g] = state_now[g] * carry + dot_tn(ended, v) * n.ones[...].astype(F32)
             keys_now[g, 0:1] = keys_now[g, 0:1] * carry + column_sum(ended.astype(F32))
-        after = n.inputs[at].astype(F32) + dot(n.context[at], weight(3))
-        centre = after - mean_last(after)
-        scale = lax.rsqrt(mean_last(centre * centre) + epsilon)
-        normal = centre * scale
-        n.normal_two[at] = normal
-        n.scale_two[at] = jnp.broadcast_to(scale, (CHUNK, 128))
-        n.normed_ffn[at] = (normal * gain_two + shift_two).astype(BF16)
-        n.result[at] = after + b_down
-
-    per_chunk(
-        [
-            [lambda: later.columns(1), lambda: later.rows_b(0)],
-            [lambda: later.columns(2), lambda: later.rows_b(1), lambda: later.rows_twin(0)],
-            [lambda: later.columns(3), lambda: later.rows_b(2), lambda: later.rows_twin(1)],
-            [lambda: later.rows_b(3), lambda: later.rows_twin(2)],
-        ],
-        forward,
-    )
-    later.rows_twin(3)
-    later.rest()
+
+        return body
+
+    per_chunk([[], [], [(lambda: gather_2.line_a(1)), (lambda: gather_1.twin(1))], []], forward(0))
+    gather_2.line_b(0)
+    gather_2.line_b(2)
+    gather_1.twin(2)
+    per_chunk([[], [(lambda: gather_1.twin(0))], [], []], forward(1))
+    gather_1.rest()
+    gather_2.line_b(1)
 
     c0 = 0.7978845608028654
     c1 = c0 * 0.044715
-    n.grad_normed[...] = jnp.zeros(n.grad_normed.shape, F32)
-
-    def ffn(i, events):
-        bias = vecs[8 + i : 9 + i]
-
+
+    def hidden_units(which):
         def body(t):
             at = rows_of(t)
-            pre = dot(n.normed_ffn[at], weight(4 + i)) + bias
-            square = pre * pre
-            half = 0.5 + 0.5 * jnp.tanh(pre * (c0 + c1 * square))
-            hidden = pre * half
-            slope = half + (2.0 * hidden) * (1.0 - half) * (c0 + (3.0 * c1) * square)
-            low = hidden.astype(BF16)
-            n.hidden[at] = low
-            n.result[at] = n.result[at] + dot(low, weight_down(i))
-            grad = (dot_nt(n.cotangent[at], weight_down(i)) * slope).astype(BF16)
-            n.grad_pre[at] = grad
+            if which == 0:
+                after = n.inputs[at].astype(F32) + dot(n.context[at], weight(3))
+                centre = after - mean_last(after)
+                scale = lax.rsqrt(mean_last(centre * centre) + epsilon)
+                normal = centre * scale
+                n.normal_two[at] = normal.astype(BF16)
+                n.scale_two[at] = jnp.broadcast_to(scale, (CHUNK, 128))
+                normed = (normal * gain_two + shift_two).astype(BF16)
+                n.normed_ffn[at] = normed
+                n.result[at] = after + b_down
+                n.grad_normed[at] = jnp.zeros((CHUNK, WIDTH), F32)
+            else:
+                normed = n.normed_ffn[at]
+            for i in (2 * which, 2 * which + 1):
+                pre = dot(normed, weight(4 + i)) + vecs[8 + i : 9 + i]
+                square = pre * pre
+                half = 0.5 + 0.5 * jnp.tanh(pre * (c0 + c1 * square))
+                hidden = pre * half
+                slope = half + (2.0 * hidden) * (1.0 - half) * (c0 + (3.0 * c1) * square)
+                cut = slice(i * WIDTH, (i + 1) * WIDTH)
+                n.hidden[at, cut] = hidden.astype(BF16)
+                n.grad_pre[at, cut] = slope.astype(BF16)
+
+        return body
+
+    per_chunk([[], [], [(lambda: gather_2.twin(1)), (lambda: gather_2.twin(0))], []], hidden_units(0))
+    per_chunk([[(lambda: gather_2.twin(2))], [gather_2.rest], [], []], hidden_units(1))
+    local[10].wait()
+    sends.finish()
+
+    def ffn(i, events):
+        cut = slice(i * WIDTH, (i + 1) * WIDTH)
+
+        def body(t):
+            at = rows_of(t)
+            n.result[at] = n.result[at] + dot(n.hidden[at, cut], weight_down(i))
+            grad = dot_nt(n.cotangent[at], weight_down(i)) * n.grad_pre[at, cut].astype(F32)
+            grad = grad.astype(BF16)
+            n.grad_pre[at, cut] = grad
             slots[0, i : i + 1] += column_sum(grad.astype(F32))
             n.grad_normed[at] = n.grad_normed[at] + dot_nt(grad, weight(4 + i))
 
         per_chunk(events, body)
         for m in range(2):
-            cut = slice(m * 256, (m + 1) * 256)
-            grad = dot_tn(n.hidden[:, cut], n.cotangent[...]).astype(BF16)
+            some = slice(i * WIDTH + m * 256, i * WIDTH + (m + 1) * 256)
+            grad = dot_tn(n.hidden[:, some], n.cotangent[...]).astype(BF16)
             part[i, m * B // 2 : (m + 1) * B // 2, :, 8 * R : 12 * R, :] = grad.reshape(
                 B // 2, 2, 4 * R, WIDTH
             )
-            grad = dot_tn(n.normed_ffn[:, cut], n.grad_pre[...]).astype(BF16)
+            some = slice(m * 256, (m + 1) * 256)
+            grad = dot_tn(n.normed_ffn[:, some], n.grad_pre[:, cut]).astype(BF16)
             part[2 * m : 2 * m + 2, :, :, (4 + i) * R : (5 + i) * R, :] = grad.reshape(
                 2, B, 2, R, WIDTH
             )
 
-    ffn(0, [])
-    ffn(1, [])
-    J[0][0]()
-    ffn(2, [[], [], [J[0][1]], []])
-    ffn(3, [[], [], [J[0][2]], []])
-    J[1][0]()
-    J[2][0]()
-    J[0][3]()
+    ffn(0, [[], [], [], []])
+    ffn(1, [[], [], [], []])
+    down_one.start()
+    ffn(2, [[], [], [up_one.start, down_one.after_core], []])
+    ffn(3, [[], [], [up_one.after_core], []])
+    up_two.start()
+    down_two.start()
 
     def norm_two_back(t):
         at = rows_of(t)
         n.output[at] = n.result[at].astype(BF16)
         grad = n.grad_normed[at]
-        normal = n.normal_two[at]
+        normal = n.normal_two[at].astype(F32)
         up = n.cotangent[at].astype(F32)
         slots[0, 4:5] += column_sum(up)
         slots[0, 7:8] += column_sum(grad * normal)
@@ -808,12 +861,15 @@
                 :, lanes[g]
             ]
 
-    per_chunk([[], [J[1][1], J[2][1]], [], []], norm_two_back)
+    per_chunk([[], [], [], []], norm_two_back)
+    down_two.after_core()
+    down_one.second()
+    store = pltpu.make_async_copy(n.output, n.output_far, n.sem_local.at[11])
+    store.start()
     for m in range(2):
         grad = dot_tn(n.context[:, m * 256 : (m + 1) * 256], n.grad_attn[...]).astype(BF16)
         part[2 * m : 2 * m + 2, :, :, 3 * R : 4 * R, :] = grad.reshape(2, B, 2, R, WIDTH)
-    J[3][0]()
-    J[0][4]()
+    up_two.after_core()
 
     def backward(g):
         state_now[g] = jnp.zeros((GROUP, GROUP), F32)
@@ -860,41 +916,55 @@
             grad = dot_tn(n.normed_attn[...], ref[:, lanes[g]]).astype(BF16)
             part[:, :, :, i * R : (i + 1) * R, lanes[g]] = grad.reshape(A, B, 2, R, GROUP)
 
-    per_chunk([[J[0][5], J[1][2], J[2][2]], [], [J[3][1]], []], backward(0), down=True)
+    per_chunk([[], [], [], []], backward(0), down=True)
+    down_one.third()
     weight_grads(0)
-    J[4][0]()
-    J[1][3]()
-    J[2][3]()
-    per_chunk([[J[4][1], J[3][2]], [J[1][4]], [J[2][4], J[3][3]], [J[4][2]]], backward(1), down=True)
+    per_chunk([[down_two.second, attn_one.start, up_one.second], [attn_one.after_core], [out_all.start], []], backward(1), down=True)
+    up_two.second()
+    down_two.third()
     weight_grads(1)
-    J[5][0]()
-    J[1][5]()
-    J[3][4]()
+    out_all.after_core()
+    attn_three.start()
 
     def norm_one_back(t):
         at = rows_of(t)
         grad = dot_nt(n.grad_query[at], weight(0))
         grad = grad + dot_nt(n.grad_key[at], weight(1))
         grad = grad + dot_nt(n.grad_value[at], weight(2))
-        normal = n.normal_one[at]
+        normal = n.normal_one[at].astype(F32)
         slots[0, 5:6] += column_sum(grad * normal)
         slots[0, 6:7] += column_sum(grad)
         e = grad * gain_one
         back = e - mean_last(e) - normal * mean_last(e * normal)
         n.grad_inputs[at] = n.grad_normed[at] + n.scale_one[at][:, 0:1] * back
 
-    per_chunk([[J[2][5], J[4][3]], [J[5][1]], [J[3][5]], []], norm_one_back)
+    per_chunk([[attn_three.after_core], [up_two.third], [out_all.second, attn_one.second, attn_two.start, attn_two.after_core], []], norm_one_back)
+    store_more = pltpu.make_async_copy(n.grad_inputs, n.grad_inputs_far, n.sem_local.at[12])
+    store_more.start()
+    up_one.third()
+    out_all.third()
+    down_one.after_a()
+    attn_two.second()
+    attn_three.second()
     T[0]()
-    J[4][4]()
     T[1]()
-    J[5][2]()
+    attn_one.third()
+    attn_two.third()
     T[2]()
-    J[4][5]()
-    J[5][3]()
+    attn_three.third()
+    up_one.after_a()
     T[3]()
-    J[5][4]()
-    for step in T[4:]:
-        step()
+    attn_two.after_a()
+    up_two.after_a()
+    out_all.after_a()
+    attn_one.after_a()
+    attn_three.after_a()
+    attn_one.finish()
+    attn_two.finish()
+    up_two.finish()
+    attn_three.finish()
+    T[4]()
+    down_one.finish()
 
     total = slots[small_sum.now]
     high = total.astype(BF16)
@@ -910,50 +980,108 @@
         picked = picked + jnp.where(keep, dot(high, pick) + dot(low, pick), 0.0)
     n.tiny_out[16:17] = column_sum(picked)
 
-    J[5][5]()
-    done = n.done
-    for i, ref in enumerate((n.out_query, n.out_key, n.out_value, n.out_out)):
+    out_all.finish()
+    up_one.finish()
+    store.wait()
+    store_more.wait()
+    sends.finish()
+
+
+PIECES = 4
+
+
+def final_kernel(output, grad_inputs, done, tiny, *refs):
+    out, grad, query, key, value, out_w, up, down = refs[:8]
+    held_out, held_grad, sem = refs[-3:]
+    rows = output.shape[0] // PIECES
+    into, back = [], []
+    for i in range(PIECES):
+        cut = pl.ds(i * rows, rows)
+        for k, (src, held, dst) in enumerate(
+            ((grad_inputs, held_grad, grad), (output, held_out, out))
+        ):
+            into.append(pltpu.make_async_copy(src.at[cut], held.at[cut], sem.at[0, k, i]))
+            back.append(pltpu.make_async_copy(held.at[cut], dst.at[cut], sem.at[1, k, i]))
+    for copy in into:
+        copy.start()
+    R = query.shape[0]
+    for i, ref in enumerate((query, key, value, out_w)):
         ref[...] = done[i * R : (i + 1) * R].astype(F32)
     for i in range(4):
-        n.out_up[:, i * WIDTH : (i + 1) * WIDTH] = done[(4 + i) * R : (5 + i) * R].astype(F32)
-    n.out_down[...] = done[8 * R : 12 * R].astype(F32)
-    sends.finish()
-
-
-def layer(reps, shards, inputs, segment_ids, weights, small, cotangent):
+        up[:, i * WIDTH : (i + 1) * WIDTH] = done[(4 + i) * R : (5 + i) * R].astype(F32)
+    down[...] = done[8 * R : 12 * R].astype(F32)
+    for ref, row in zip(refs[8:14], (16, 4, 5, 6, 7, 8), strict=True):
+        ref[...] = tiny[row, : ref.shape[0]]
+    for one, two in zip(into, back, strict=True):
+        one.wait()
+        two.start()
+    for copy in back:
+        copy.wait()
+
+
+def final(output, grad_inputs, done, tiny):
+    R = done.shape[0] // 12
+    vmem, far = pl.BlockSpec(memory_space=pltpu.VMEM), pl.BlockSpec(memory_space=pl.ANY)
+    shapes = [(output.shape, BF16), (grad_inputs.shape, F32)] + [((R, WIDTH), F32)] * 4
+    shapes += [((R, 4 * WIDTH), F32), ((4 * R, WIDTH), F32), ((4 * R,), F32)] + [((R,), F32)] * 5
+    return pl.pallas_call(
+        final_kernel,
+        out_shape=tuple(jax.ShapeDtypeStruct(*shape) for shape in shapes),
+        in_specs=[far, far, vmem, vmem],
+        out_specs=(far, far) + (vmem,) * 12,
+        scratch_shapes=[
+            pltpu.VMEM(output.shape, BF16),
+            pltpu.VMEM(grad_inputs.shape, F32),
+            pltpu.SemaphoreType.DMA((2, 2, PIECES)),
+        ],
+        name="final",
+    )(output, grad_inputs, done, tiny)
+
+
+def layer(reps, shards, inputs, segment_ids, weights, vectors, cotangent):
     length = inputs.shape[0]
     A, B = 4, shards // 8
     R = weights[0].shape[0]
     rows = 12 * R
     bits = max(reps.bit_length() - 2, 0)
     copies, n_slots = SmallReduce.counts(reps, shards)
-    n_sems = Reduce.n_sems(reps, shards)
+    sums = 5 * (2 * B + A + bits) + 2 * (3 * B - 1 + A + bits) + 1 * (3 * B - 1)
+    groups = 3
     w_query, w_key, w_value, w_out, w_up, w_down = weights
-    ins = dict(
-        inputs=inputs,
-        segment_ids=segment_ids,
+    b_up, b_down, gain_attn, shift_attn, gain_ffn, shift_ffn = vectors
+    far_ins = dict(
+        inputs_far=inputs,
+        cotangent_far=cotangent,
         w_query=w_query,
         w_key=w_key,
         w_value=w_value,
         w_out=w_out,
         w_up=w_up,
         w_down=w_down,
-        small=small,
-        cotangent=cotangent,
+    )
+    ins = dict(
+        segment_ids=segment_ids,
+        b_up=b_up,
+        b_down=b_down,
+        gain_attn=gain_attn,
+        shift_attn=shift_attn,
+        gain_ffn=gain_ffn,
+        shift_ffn=shift_ffn,
+    )
+    far_outs = dict(
+        output_far=((length, WIDTH), BF16),
+        grad_inputs_far=((length, WIDTH), F32),
     )
     outs = dict(
-        output=((length, WIDTH), BF16),
-        grad_inputs=((length, WIDTH), F32),
-        out_query=((R, WIDTH), F32),
-        out_key=((R, WIDTH), F32),
-        out_value=((R, WIDTH), F32),
-        out_out=((R, WIDTH), F32),
-        out_up=((R, 4 * WIDTH), F32),
-        out_down=((4 * R, WIDTH), F32),
+        done=((rows, WIDTH), BF16),
         tiny_out=((24, 128), F32),
     )
     tall = (length, WIDTH)
     buffers = dict(
+        inputs=(tall, BF16),
+        cotangent=(tall, BF16),
+        output=(tall, BF16),
+        grad_inputs=(tall, F32),
         full=((A, B, 2, rows, WIDTH), BF16),
         part=((A, B, 2, rows, WIDTH), BF16),
         core=((A, B, rows, WIDTH), BF16),
@@ -961,7 +1089,6 @@
         pair=((A, B, rows, WIDTH), BF16),
         line_a=((A - 1, rows, WIDTH), BF16),
         wide=((max(2 * bits, 1), rows if bits else 16, WIDTH), BF16),
-        done=((rows, WIDTH), BF16),
         smalls=((A, B, 2, 8, 128), F32),
         slots=((n_slots, 16, WIDTH), F32),
         vecs=((16, WIDTH), F32),
@@ -970,7 +1097,7 @@
         ones=((GROUP, GROUP), BF16),
         mask=((length // CHUNK, CHUNK, CHUNK), BF16),
         mask_t=((length // CHUNK, CHUNK, CHUNK), BF16),
-        normal_one=(tall, F32),
+        normal_one=(tall, BF16),
         scale_one=((length, 128), F32),
         normed_attn=(tall, BF16),
         query=(tall, BF16),
@@ -982,42 +1109,45 @@
         state=((GROUPS, length // CHUNK, GROUP, GROUP), BF16),
         state_now=((GROUPS, GROUP, GROUP), F32),
         keys_now=((GROUPS, 8, GROUP), F32),
-        normal_two=(tall, F32),
+        normal_two=(tall, BF16),
         scale_two=((length, 128), F32),
         normed_ffn=(tall, BF16),
-        hidden=(tall, BF16),
-        grad_pre=(tall, BF16),
+        hidden=((length, 4 * WIDTH), BF16),
+        grad_pre=((length, 4 * WIDTH), BF16),
         grad_normed=(tall, F32),
         grad_attn=(tall, BF16),
         grad_mixed=(tall, BF16),
         grad_totals=(tall, F32),
     )
     sems = dict(
-        sem_local=(9,),
+        sem_local=(13,),
         send0=(A + B,),
         recv0=(A + B,),
-        send1=(2, A, B, 7),
-        recv1=(2, A, B, 2, 2),
-        send2=(6, n_sems),
-        recv2=(6, n_sems),
+        send1=(max(groups * Gather.n_sems(shards), sums),),
+        recv1=(groups * Gather.n_sems(shards),),
+        recv2=(sums,),
         send3=(copies,),
         recv3=(copies,),
     )
-    names = list(ins) + list(outs) + list(buffers) + list(sems)
+    names = [*far_ins, *ins, *far_outs, *outs, *buffers, *sems]
 
     def kernel(*refs):
         n = types.SimpleNamespace(**dict(zip(names, refs, strict=True)))
         n.result = n.grad_inputs
-        n.grad_query, n.grad_key, n.grad_value = n.hidden, n.grad_pre, n.normed_ffn
+        n.grad_query, n.grad_key, n.grad_value = (
+            n.hidden.at[:, pl.ds(i * WIDTH, WIDTH)] for i in range(3)
+        )
         layer_kernel(reps, shards, length, n)
 
-    vmem = pl.BlockSpec(memory_space=pltpu.VMEM)
+    vmem, far = pl.BlockSpec(memory_space=pltpu.VMEM), pl.BlockSpec(memory_space=pl.ANY)
     flops = 2 * 3 * length * WIDTH * WIDTH * 12 + 20 * length * length * WIDTH
-    results = pl.pallas_call(
+    return pl.pallas_call(
         kernel,
-        out_shape=tuple(jax.ShapeDtypeStruct(*spec) for spec in outs.values()),
-        in_specs=[vmem] * len(ins),
-        out_specs=(vmem,) * len(outs),
+        out_shape=tuple(
+            jax.ShapeDtypeStruct(*spec) for spec in [*far_outs.values(), *outs.values()]
+        ),
+        in_specs=[far] * len(far_ins) + [vmem] * len(ins),
+        out_specs=(far,) * len(far_outs) + (vmem,) * len(outs),
         scratch_shapes=[pltpu.VMEM(*spec) for spec in buffers.values()]
         + [pltpu.SemaphoreType.DMA(shape) for shape in sems.values()],
         compiler_params=pltpu.CompilerParams(
@@ -1025,8 +1155,7 @@
         ),
         cost_estimate=pl.CostEstimate(flops=flops, bytes_accessed=8 << 20, transcendentals=0),
         name="layer",
-    )(*ins.values())
-    return dict(zip(outs, results, strict=True))
+    )(*far_ins.values(), *ins.values())
 
 
 def on_device(
@@ -1049,38 +1178,17 @@
     cotangent,
 ):
     sequences, length, width = inputs.shape
-    R = w_query.shape[0]
-
-    def padded(vec):
-        return jnp.pad(vec.astype(F32), (0, 128 - vec.shape[0]))[None]
-
-    small = jnp.concatenate(
-        [padded(v) for v in (b_up, b_down, gain_attn, shift_attn, gain_ffn, shift_ffn)]
-        + [jnp.zeros((2, 128), F32)],
-        axis=0,
-    )
-    got = layer(
+    output, grad_inputs, done, tiny = layer(
         reps,
         shards,
         inputs.reshape(sequences * length, width),
         segment_ids,
         (w_query, w_key, w_value, w_out, w_up, w_down),
-        small,
+        (b_up, b_down, gain_attn, shift_attn, gain_ffn, shift_ffn),
         cotangent.reshape(sequences * length, width),
     )
-    tiny = got["tiny_out"]
-    return (
-        got["output"].reshape(inputs.shape),
-        got["grad_inputs"].reshape(inputs.shape),
-        got["out_query"],
-        got["out_key"],
-        got["out_value"],
-        got["out_out"],
-        got["out_up"],
-        got["out_down"],
-        tiny[16, : 4 * R],
-        *(tiny[i, :R] for i in range(4, 9)),
-    )
+    output, grad_inputs, *grads = final(output, grad_inputs, done, tiny)
+    return (output.reshape(inputs.shape), grad_inputs.reshape(inputs.shape), *grads)
 
 
 def solution(mesh):

time: 147 us -> 114 us (0.78)
  Pallas kernels: 133 us -> 113 us
  local copies, waits for them, and re-layouts: 10.7 us -> 0 us
  other arithmetic: 2.03 us -> 0 us
    pallas_call x1, Pallas kernels: 133 us -> 108 us  [layer(): pl.pallas_call(kernel, out_shape=tuple((jax.ShapeDtypeStruct(*spec) for s...]
    unnamed x22 -> x0, local copies, waits for them, and re-layouts: 7.53 us -> none
    pallas_call x0 -> x1, Pallas kernels: none -> 4.73 us  [final(): pl.pallas_call(final_kernel, out_shape=tuple((jax.ShapeDtypeStruct(*shape...]
    squeeze x2 -> x0, local copies, waits for them, and re-layouts: 2.56 us -> none  [the longest x1 1.38 us: on_device(): tiny[i, :R]]
    broadcast_in_dim x3 -> x0, other arithmetic: 2.03 us -> none  [padded(): return jnp.pad(vec.astype(F32), (0, 128 - vec.shape[0]))[None]]
where the time goes in v2:
time: 114 us; the launch traced here: 113 us
  Pallas kernels  113 us (99%)
    pallas_call x1, Pallas kernels, layer(): pl.pallas_call(kernel, out_shape=tuple((jax.ShapeDtypeStruct(*spec) for s...  108 us
    pallas_call x1, Pallas kernels, final(): pl.pallas_call(final_kernel, out_shape=tuple((jax.ShapeDtypeStruct(*shape...  4.73 us

profile of v2, /device:TPU:0, one launch (start us, length us, event | category | flops | bytes accessed | tf_op | source)
XLA Modules:
  0.0 113.4 jit_solution(10289351665665639398)
XLA Ops:
  0.7 107.8 %layer.1 = (bf16[1024,512]{1,0:T(8,128)(2,1)}, f32[1024,512]{1,0:T(8,128)}, bf16[384,512]{1,0:T(8,128)(2,1)}, f32[24,128]{1,0:T(8,128)}) custom-call(bf16[1024,512]{1,0:T(8,128)(2,1)} %bitcast.5, bf16[1024,512]{1,0:T(8,128)(2,1)} %bitcast.6, bf16[32,512]{1,0:T(8,128)(2,1)} %refs_2_.1, bf16[32,512]{1,0:T(8,128)(2,1)} %refs_3_.1, bf16[32,512]{1,0:T(8,128)(2,1)} %refs_4_.1, ...), custom_call_target="tpu_custom_call" | custom-call | flops 30064771072 | bytes 8388608 | tf_op jit(solution)/shard_map/layer/pallas_call | solution.py:1144
  108.5 4.7 %final.1 = (bf16[1024,512]{1,0:T(8,128)(2,1)}, f32[1024,512]{1,0:T(8,128)}, f32[32,512]{1,0:T(8,128)}, f32[32,512]{1,0:T(8,128)}, f32[32,512]{1,0:T(8,128)}, /*i...) custom-call(bf16[1024,512]{1,0:T(8,128)(2,1)} %get-tuple-element.32., ...), custom_call_target="tpu_custom_call" | custom-call | tf_op jit(solution)/shard_map/final/pallas_call | solution.py:1027

commit v3 on v2

--- a/solution.py
+++ b/solution.py
@@ -591,7 +591,7 @@
     def job(lo, rows, at=0, lanes=WIDTH, **more):
         base = sum(one.n_sems() for one in made)
         window = (lo * R, rows * R, at, lanes)
-        made.append(Reduce(p, part, bufs, window, (n.send1, n.recv2), base, sends, **more))
+        made.append(Reduce(p, part, bufs, window, (n.send2, n.recv2), base, sends, **more))
         return made[-1]
 
     up_one = job(4, 2)
@@ -624,16 +624,20 @@
 
         lax.fori_loop(0, chunks, step, 0)
 
+    tiny.own()
     gather_0.own()
-    gather_0.line_b_own()
+    tiny.second()
     gather_1.own()
     gather_0.line_a(1)
     gather_0.line_a(2)
     gather_0.line_a(0)
+    gather_0.line_b(1)
+    tiny.third()
+    gather_1.line_b_own()
+    gather_0.line_b(2)
+    gather_2.own()
+    gather_0.line_b_own()
     gather_0.line_b(0)
-    gather_0.line_b(2)
-    gather_1.line_b_own()
-    gather_2.own()
 
     seg_row = n.segment_ids[...].astype(F32)
     seg_rows = n.seg_rows
@@ -663,9 +667,10 @@
     def flags(one, two):
         return twice(jnp.where(one == two, 1.0, 0.0))
 
-    tiny.own()
-    gather_0.line_b(1)
-    gather_1.line_a(2)
+    tiny.last()
+    gather_0.twin(2)
+    gather_1.line_a(1)
+    gather_0.twin(1)
 
     local[9].wait()
     def norm_one(t):
@@ -677,21 +682,8 @@
         n.scale_one[at] = jnp.broadcast_to(scale, (CHUNK, 128))
 
     per_chunk([], norm_one)
-    gather_1.line_a(1)
-    tiny.second()
-    gather_0.twin(2)
-    gather_1.line_b(2)
-    gather_1.line_a(0)
-    gather_1.line_b(1)
     gather_0.twin(0)
-    gather_0.twin(1)
-    gather_0.rest()
-    tiny.third()
-    tiny.last()
-    gather_2.line_a(0)
-    gather_2.line_b_own()
-    gather_2.line_a(2)
-    gather_1.line_b(0)
+    gather_1.line_a(2)
 
     blocks = smalls[...].reshape(shards * 8, 128).astype(BF16)
     lane = iota((128, WIDTH), 1)
@@ -708,6 +700,7 @@
         vecs[8 + i : 9 + i] = jnp.sum(picked, axis=0)[0:1]
     b_down, gain_one, shift_one, gain_two, shift_two = (vecs[i : i + 1] for i in range(1, 6))
 
+    gather_0.rest()
 
     def weight(i):
         return full[:, :, :, i * R : (i + 1) * R, :].reshape(WIDTH, WIDTH)
@@ -760,13 +753,11 @@
 
         return body
 
-    per_chunk([[], [], [(lambda: gather_2.line_a(1)), (lambda: gather_1.twin(1))], []], forward(0))
+    per_chunk([[(lambda: gather_1.line_b(1)), gather_2.line_b_own, (lambda: gather_1.line_a(0))], [(lambda: gather_1.line_b(2))], [(lambda: gather_2.line_a(0))], []], forward(0))
+    gather_1.line_b(0)
+    per_chunk([[], [(lambda: gather_1.twin(2))], [(lambda: gather_1.twin(1)), (lambda: gather_2.line_a(2)), (lambda: gather_1.twin(0)), (lambda: gather_2.line_a(1))], []], forward(1))
     gather_2.line_b(0)
-    gather_2.line_b(2)
-    gather_1.twin(2)
-    per_chunk([[], [(lambda: gather_1.twin(0))], [], []], forward(1))
     gather_1.rest()
-    gather_2.line_b(1)
 
     c0 = 0.7978845608028654
     c1 = c0 * 0.044715
@@ -784,7 +775,6 @@
                 normed = (normal * gain_two + shift_two).astype(BF16)
                 n.normed_ffn[at] = normed
                 n.result[at] = after + b_down
-                n.grad_normed[at] = jnp.zeros((CHUNK, WIDTH), F32)
             else:
                 normed = n.normed_ffn[at]
             for i in (2 * which, 2 * which + 1):
@@ -799,48 +789,59 @@
 
         return body
 
-    per_chunk([[], [], [(lambda: gather_2.twin(1)), (lambda: gather_2.twin(0))], []], hidden_units(0))
-    per_chunk([[(lambda: gather_2.twin(2))], [gather_2.rest], [], []], hidden_units(1))
+    per_chunk([[], [], [(lambda: gather_2.line_b(1))], []], hidden_units(0))
+    per_chunk([[(lambda: gather_2.line_b(2))], [], [], []], hidden_units(1))
     local[10].wait()
-    sends.finish()
-
-    def ffn(i, events):
-        cut = slice(i * WIDTH, (i + 1) * WIDTH)
-
-        def body(t):
-            at = rows_of(t)
-            n.result[at] = n.result[at] + dot(n.hidden[at, cut], weight_down(i))
-            grad = dot_nt(n.cotangent[at], weight_down(i)) * n.grad_pre[at, cut].astype(F32)
-            grad = grad.astype(BF16)
-            n.grad_pre[at, cut] = grad
-            slots[0, i : i + 1] += column_sum(grad.astype(F32))
-            n.grad_normed[at] = n.grad_normed[at] + dot_nt(grad, weight(4 + i))
-
-        per_chunk(events, body)
+
+    def down_grads(i):
         for m in range(2):
             some = slice(i * WIDTH + m * 256, i * WIDTH + (m + 1) * 256)
             grad = dot_tn(n.hidden[:, some], n.cotangent[...]).astype(BF16)
             part[i, m * B // 2 : (m + 1) * B // 2, :, 8 * R : 12 * R, :] = grad.reshape(
                 B // 2, 2, 4 * R, WIDTH
             )
+
+    down_grads(0)
+    gather_2.twin(2)
+    down_grads(1)
+    gather_2.twin(0)
+    gather_2.twin(1)
+    down_grads(2)
+    down_grads(3)
+    gather_2.rest()
+
+    def ffn(i, events):
+        cut = slice(i * WIDTH, (i + 1) * WIDTH)
+
+        def body(t):
+            at = rows_of(t)
+            grad = dot_nt(n.cotangent[at], weight_down(i)) * n.grad_pre[at, cut].astype(F32)
+            grad = grad.astype(BF16)
+            n.grad_pre[at, cut] = grad
+            slots[0, i : i + 1] += column_sum(grad.astype(F32))
+
+        per_chunk(events, body)
+        for m in range(2):
             some = slice(m * 256, (m + 1) * 256)
             grad = dot_tn(n.normed_ffn[:, some], n.grad_pre[:, cut]).astype(BF16)
             part[2 * m : 2 * m + 2, :, :, (4 + i) * R : (5 + i) * R, :] = grad.reshape(
                 2, B, 2, R, WIDTH
             )
 
-    ffn(0, [[], [], [], []])
+    ffn(0, [[down_two.start], [], [], []])
+    down_one.start()
     ffn(1, [[], [], [], []])
-    down_one.start()
-    ffn(2, [[], [], [up_one.start, down_one.after_core], []])
-    ffn(3, [[], [], [up_one.after_core], []])
+    up_one.start()
+    ffn(2, [[], [], [], [down_one.after_core]])
+    ffn(3, [[], [up_one.after_core], [], []])
     up_two.start()
-    down_two.start()
+    down_two.after_core()
 
     def norm_two_back(t):
         at = rows_of(t)
-        n.output[at] = n.result[at].astype(BF16)
-        grad = n.grad_normed[at]
+        grad = dot_nt(n.grad_pre[at, 0:WIDTH], weight(4))
+        for i in range(1, 4):
+            grad = grad + dot_nt(n.grad_pre[at, i * WIDTH : (i + 1) * WIDTH], weight(4 + i))
         normal = n.normal_two[at].astype(F32)
         up = n.cotangent[at].astype(F32)
         slots[0, 4:5] += column_sum(up)
@@ -861,15 +862,10 @@
                 :, lanes[g]
             ]
 
-    per_chunk([[], [], [], []], norm_two_back)
-    down_two.after_core()
-    down_one.second()
-    store = pltpu.make_async_copy(n.output, n.output_far, n.sem_local.at[11])
-    store.start()
+    per_chunk([[up_two.after_core], [], [], []], norm_two_back)
     for m in range(2):
         grad = dot_tn(n.context[:, m * 256 : (m + 1) * 256], n.grad_attn[...]).astype(BF16)
         part[2 * m : 2 * m + 2, :, :, 3 * R : 4 * R, :] = grad.reshape(2, B, 2, R, WIDTH)
-    up_two.after_core()
 
     def backward(g):
         state_now[g] = jnp.zeros((GROUP, GROUP), F32)
@@ -916,15 +912,16 @@
             grad = dot_tn(n.normed_attn[...], ref[:, lanes[g]]).astype(BF16)
             part[:, :, :, i * R : (i + 1) * R, lanes[g]] = grad.reshape(A, B, 2, R, GROUP)
 
-    per_chunk([[], [], [], []], backward(0), down=True)
-    down_one.third()
+    per_chunk([[], [down_one.second, out_all.start, up_one.second, down_two.second], [], []], backward(0), down=True)
     weight_grads(0)
-    per_chunk([[down_two.second, attn_one.start, up_one.second], [attn_one.after_core], [out_all.start], []], backward(1), down=True)
-    up_two.second()
-    down_two.third()
+    attn_one.start()
+    per_chunk([[up_one.third, attn_one.after_core, up_two.second], [down_two.third, down_one.third], [], []], backward(1), down=True)
     weight_grads(1)
+    attn_one.second()
     out_all.after_core()
     attn_three.start()
+    up_two.third()
+    attn_two.start()
 
     def norm_one_back(t):
         at = rows_of(t)
@@ -936,35 +933,37 @@
         slots[0, 6:7] += column_sum(grad)
         e = grad * gain_one
         back = e - mean_last(e) - normal * mean_last(e * normal)
-        n.grad_inputs[at] = n.grad_normed[at] + n.scale_one[at][:, 0:1] * back
-
-    per_chunk([[attn_three.after_core], [up_two.third], [out_all.second, attn_one.second, attn_two.start, attn_two.after_core], []], norm_one_back)
-    store_more = pltpu.make_async_copy(n.grad_inputs, n.grad_inputs_far, n.sem_local.at[12])
+        n.grad_normed[at] = n.grad_normed[at] + n.scale_one[at][:, 0:1] * back
+
+    per_chunk([[], [attn_three.after_core], [], []], norm_one_back)
+    store = pltpu.make_async_copy(n.grad_normed, n.grad_inputs_far, n.sem_local.at[11])
+    store.start()
+    T[0]()
+    attn_two.after_core()
+    out_all.second()
+    attn_one.third()
+    T[1]()
+    attn_three.second()
+    attn_two.second()
+
+    def outputs(t):
+        at = rows_of(t)
+        total = n.result[at]
+        for i in range(4):
+            total = total + dot(n.hidden[at, i * WIDTH : (i + 1) * WIDTH], weight_down(i))
+        n.output[at] = total.astype(BF16)
+
+    per_chunk([[out_all.third, T[2], up_two.after_a, down_one.after_a, up_one.after_a, attn_two.third], [attn_three.third, T[3], out_all.after_a, attn_one.after_a], [], []], outputs)
+    store_more = pltpu.make_async_copy(n.output, n.output_far, n.sem_local.at[12])
     store_more.start()
-    up_one.third()
-    out_all.third()
-    down_one.after_a()
-    attn_two.second()
-    attn_three.second()
-    T[0]()
-    T[1]()
-    attn_one.third()
-    attn_two.third()
-    T[2]()
-    attn_three.third()
-    up_one.after_a()
-    T[3]()
+    attn_three.after_a()
+    down_one.finish()
+    up_one.finish()
+    attn_one.finish()
+    out_all.finish()
     attn_two.after_a()
-    up_two.after_a()
-    out_all.after_a()
-    attn_one.after_a()
-    attn_three.after_a()
-    attn_one.finish()
-    attn_two.finish()
     up_two.finish()
-    attn_three.finish()
     T[4]()
-    down_one.finish()
 
     total = slots[small_sum.now]
     high = total.astype(BF16)
@@ -980,8 +979,8 @@
         picked = picked + jnp.where(keep, dot(high, pick) + dot(low, pick), 0.0)
     n.tiny_out[16:17] = column_sum(picked)
 
-    out_all.finish()
-    up_one.finish()
+    attn_three.finish()
+    attn_two.finish()
     store.wait()
     store_more.wait()
     sends.finish()
@@ -991,28 +990,38 @@
 
 
 def final_kernel(output, grad_inputs, done, tiny, *refs):
-    out, grad, query, key, value, out_w, up, down = refs[:8]
-    held_out, held_grad, sem = refs[-3:]
+    outs = refs[:14]
+    held_out, held_grad, held_done, held_tiny = refs[14:18]
+    held = refs[18:-2]
+    sem, more = refs[-2:]
     rows = output.shape[0] // PIECES
+    first = [
+        pltpu.make_async_copy(done, held_done, more.at[0]),
+        pltpu.make_async_copy(tiny, held_tiny, more.at[1]),
+    ]
     into, back = [], []
     for i in range(PIECES):
         cut = pl.ds(i * rows, rows)
-        for k, (src, held, dst) in enumerate(
-            ((grad_inputs, held_grad, grad), (output, held_out, out))
+        for k, (src, mid, dst) in enumerate(
+            ((grad_inputs, held_grad, outs[1]), (output, held_out, outs[0]))
         ):
-            into.append(pltpu.make_async_copy(src.at[cut], held.at[cut], sem.at[0, k, i]))
-            back.append(pltpu.make_async_copy(held.at[cut], dst.at[cut], sem.at[1, k, i]))
-    for copy in into:
+            into.append(pltpu.make_async_copy(src.at[cut], mid.at[cut], sem.at[0, k, i]))
+            back.append(pltpu.make_async_copy(mid.at[cut], dst.at[cut], sem.at[1, k, i]))
+    for copy in first + into:
         copy.start()
-    R = query.shape[0]
-    for i, ref in enumerate((query, key, value, out_w)):
-        ref[...] = done[i * R : (i + 1) * R].astype(F32)
+    for copy in first:
+        copy.wait()
+    R = held[0].shape[0]
     for i in range(4):
-        up[:, i * WIDTH : (i + 1) * WIDTH] = done[(4 + i) * R : (5 + i) * R].astype(F32)
-    down[...] = done[8 * R : 12 * R].astype(F32)
-    for ref, row in zip(refs[8:14], (16, 4, 5, 6, 7, 8), strict=True):
-        ref[...] = tiny[row, : ref.shape[0]]
-    for one, two in zip(into, back, strict=True):
+        held[i][...] = held_done[i * R : (i + 1) * R].astype(F32)
+        held[4][:, i * WIDTH : (i + 1) * WIDTH] = held_done[(4 + i) * R : (5 + i) * R].astype(F32)
+    held[5][...] = held_done[8 * R : 12 * R].astype(F32)
+    for i in range(6):
+        back.append(pltpu.make_async_copy(held[i], outs[2 + i], more.at[2 + i]))
+        back[-1].start()
+    for ref, row in zip(outs[8:14], (16, 4, 5, 6, 7, 8), strict=True):
+        ref[...] = held_tiny[row, : ref.shape[0]]
+    for one, two in zip(into, back, strict=False):
         one.wait()
         two.start()
     for copy in back:
@@ -1022,18 +1031,22 @@
 def final(output, grad_inputs, done, tiny):
     R = done.shape[0] // 12
     vmem, far = pl.BlockSpec(memory_space=pltpu.VMEM), pl.BlockSpec(memory_space=pl.ANY)
-    shapes = [(output.shape, BF16), (grad_inputs.shape, F32)] + [((R, WIDTH), F32)] * 4
-    shapes += [((R, 4 * WIDTH), F32), ((4 * R, WIDTH), F32), ((4 * R,), F32)] + [((R,), F32)] * 5
+    grads = [((R, WIDTH), F32)] * 4 + [((R, 4 * WIDTH), F32), ((4 * R, WIDTH), F32)]
+    shapes = [(output.shape, BF16), (grad_inputs.shape, F32)] + grads
+    shapes += [((4 * R,), F32)] + [((R,), F32)] * 5
     return pl.pallas_call(
         final_kernel,
         out_shape=tuple(jax.ShapeDtypeStruct(*shape) for shape in shapes),
-        in_specs=[far, far, vmem, vmem],
-        out_specs=(far, far) + (vmem,) * 12,
+        in_specs=[far] * 4,
+        out_specs=(far,) * 8 + (vmem,) * 6,
         scratch_shapes=[
             pltpu.VMEM(output.shape, BF16),
             pltpu.VMEM(grad_inputs.shape, F32),
-            pltpu.SemaphoreType.DMA((2, 2, PIECES)),
-        ],
+            pltpu.VMEM(done.shape, BF16),
+            pltpu.VMEM(tiny.shape, F32),
+        ]
+        + [pltpu.VMEM(*shape) for shape in grads]
+        + [pltpu.SemaphoreType.DMA((2, 2, PIECES)), pltpu.SemaphoreType.DMA((8,))],
         name="final",
     )(output, grad_inputs, done, tiny)
 
@@ -1081,7 +1094,7 @@
         inputs=(tall, BF16),
         cotangent=(tall, BF16),
         output=(tall, BF16),
-        grad_inputs=(tall, F32),
+        result=(tall, F32),
         full=((A, B, 2, rows, WIDTH), BF16),
         part=((A, B, 2, rows, WIDTH), BF16),
         core=((A, B, rows, WIDTH), BF16),
@@ -1123,8 +1136,9 @@
         sem_local=(13,),
         send0=(A + B,),
         recv0=(A + B,),
-        send1=(max(groups * Gather.n_sems(shards), sums),),
+        send1=(groups * Gather.n_sems(shards),),
         recv1=(groups * Gather.n_sems(shards),),
+        send2=(sums,),
         recv2=(sums,),
         send3=(copies,),
         recv3=(copies,),
@@ -1133,9 +1147,8 @@
 
     def kernel(*refs):
         n = types.SimpleNamespace(**dict(zip(names, refs, strict=True)))
-        n.result = n.grad_inputs
         n.grad_query, n.grad_key, n.grad_value = (
-            n.hidden.at[:, pl.ds(i * WIDTH, WIDTH)] for i in range(3)
+            n.grad_pre.at[:, pl.ds(i * WIDTH, WIDTH)] for i in range(3)
         )
         layer_kernel(reps, shards, length, n)
 

time: 114 us -> 105 us (0.921)
  Pallas kernels: 113 us -> 104 us
    pallas_call x1, Pallas kernels: 108 us -> 99.4 us  [layer(): pl.pallas_call(kernel, out_shape=tuple((jax.ShapeDtypeStruct(*spec) for s...]
where the time goes in v3:
time: 105 us
  Pallas kernels  104 us (99%)
    pallas_call x1, Pallas kernels, layer(): pl.pallas_call(kernel, out_shape=tuple((jax.ShapeDtypeStruct(*spec) for s...  99.4 us
    pallas_call x1, Pallas kernels, final(): pl.pallas_call(final_kernel, out_shape=tuple((jax.ShapeDtypeStruct(*shape...  4.42 us

profile of v3, /device:TPU:0, one launch (start us, length us, event | category | flops | bytes accessed | tf_op | source)
XLA Modules:
  0.0 104.6 jit_solution(7817616949992210666)
XLA Ops:
  0.7 99.4 %layer.1 = (bf16[1024,512]{1,0:T(8,128)(2,1)}, f32[1024,512]{1,0:T(8,128)}, bf16[384,512]{1,0:T(8,128)(2,1)}, f32[24,128]{1,0:T(8,128)}) custom-call(bf16[1024,512]{1,0:T(8,128)(2,1)} %bitcast.5, bf16[1024,512]{1,0:T(8,128)(2,1)} %bitcast.6, bf16[32,512]{1,0:T(8,128)(2,1)} %refs_2_.1, bf16[32,512]{1,0:T(8,128)(2,1)} %refs_3_.1, bf16[32,512]{1,0:T(8,128)(2,1)} %refs_4_.1, ...), custom_call_target="tpu_custom_call" | custom-call | flops 30064771072 | bytes 8388608 | tf_op jit(solution)/shard_map/layer/pallas_call | solution.py:1157
  100.0 4.4 %final.1 = (bf16[1024,512]{1,0:T(8,128)(2,1)}, f32[1024,512]{1,0:T(8,128)}, f32[32,512]{1,0:T(8,128)}, f32[32,512]{1,0:T(8,128)}, f32[32,512]{1,0:T(8,128)}, /*i...) custom-call(bf16[1024,512]{1,0:T(8,128)(2,1)} %get-tuple-element.32., ...), custom_call_target="tpu_custom_call" | custom-call | tf_op jit(solution)/shard_map/final/pallas_call | solution.py:1037

commit v4 on v3

--- a/solution.py
+++ b/solution.py
@@ -595,9 +595,9 @@
         return made[-1]
 
     up_one = job(4, 2)
-    up_two = job(6, 2)
+    up_two = job(6, 2, pair_first=True)
     down_one = job(8, 4, pair_first=True, span=(0, 2))
-    down_two = job(8, 4, pair_first=True, span=(2, 4), end=down_one)
+    down_two = job(8, 4, span=(2, 4), end=down_one)
     out_all = job(3, 1)
     attn_one = job(0, 3, 0, 256)
     attn_two = job(0, 1, 256, 256)
@@ -606,10 +606,12 @@
     small_sum = SmallReduce(p, slots, n.send3, n.recv3, sends)
     T = small_sum.steps()
 
-    def rows_of(t):
-        return pl.ds(pl.multiple_of(t * CHUNK, CHUNK), CHUNK)
-
-    def per_chunk(events, body, down=False):
+    def rows_of(t, size=CHUNK):
+        return pl.ds(pl.multiple_of(t * size, size), size)
+
+    def per_chunk(events, body, down=False, size=CHUNK):
+        chunks = length // size
+
         def step(i, carry):
             body(chunks - 1 - i if down else i)
             for at, calls in enumerate(events):
@@ -629,15 +631,6 @@
     tiny.second()
     gather_1.own()
     gather_0.line_a(1)
-    gather_0.line_a(2)
-    gather_0.line_a(0)
-    gather_0.line_b(1)
-    tiny.third()
-    gather_1.line_b_own()
-    gather_0.line_b(2)
-    gather_2.own()
-    gather_0.line_b_own()
-    gather_0.line_b(0)
 
     seg_row = n.segment_ids[...].astype(F32)
     seg_rows = n.seg_rows
@@ -667,10 +660,11 @@
     def flags(one, two):
         return twice(jnp.where(one == two, 1.0, 0.0))
 
+    tiny.third()
+    gather_0.line_a(2)
     tiny.last()
-    gather_0.twin(2)
-    gather_1.line_a(1)
-    gather_0.twin(1)
+    gather_0.line_a(0)
+    gather_0.line_b(1)
 
     local[9].wait()
     def norm_one(t):
@@ -682,7 +676,14 @@
         n.scale_one[at] = jnp.broadcast_to(scale, (CHUNK, 128))
 
     per_chunk([], norm_one)
-    gather_0.twin(0)
+    gather_0.line_b(2)
+    gather_1.line_a(1)
+    gather_0.twin(2)
+    gather_1.line_a(0)
+    gather_0.twin(1)
+    gather_0.line_b(0)
+    gather_1.line_b(1)
+    gather_0.line_b_own()
     gather_1.line_a(2)
 
     blocks = smalls[...].reshape(shards * 8, 128).astype(BF16)
@@ -700,6 +701,8 @@
         vecs[8 + i : 9 + i] = jnp.sum(picked, axis=0)[0:1]
     b_down, gain_one, shift_one, gain_two, shift_two = (vecs[i : i + 1] for i in range(1, 6))
 
+    gather_2.own()
+    gather_0.twin(0)
     gather_0.rest()
 
     def weight(i):
@@ -714,23 +717,20 @@
     keys_now[...] = jnp.zeros(keys_now.shape, F32)
     slots[0] = jnp.zeros(slots.shape[1:], F32)
 
+    def project(t):
+        at = rows_of(t, 512)
+        normed = (n.normal_one[at].astype(F32) * gain_one + shift_one).astype(BF16)
+        n.normed_attn[at] = normed
+        n.query[at] = feature(dot(normed, weight(0))).astype(BF16)
+        n.key[at] = feature(dot(normed, weight(1))).astype(BF16)
+        n.value[at] = dot(normed, weight(2)).astype(BF16)
+
     def forward(g):
         cut = lanes[g]
 
-        def weight_part(i):
-            return full[:, :, :, i * R : (i + 1) * R, cut].reshape(WIDTH, GROUP)
-
         def body(t):
             at = rows_of(t)
-            if g == 0:
-                normed = (n.normal_one[at].astype(F32) * gain_one + shift_one).astype(BF16)
-                n.normed_attn[at] = normed
-            else:
-                normed = n.normed_attn[at]
-            q = feature(dot(normed, weight_part(0))).astype(BF16)
-            k = feature(dot(normed, weight_part(1))).astype(BF16)
-            v = dot(normed, weight_part(2)).astype(BF16)
-            n.query[at, cut], n.key[at, cut], n.value[at, cut] = q, k, v
+            q, k, v = n.query[at, cut], n.key[at, cut], n.value[at, cut]
             seg = seg_chunk(t)
             before = flags(seg, seg_at(t, -1))
             ending = flags(seg, seg_at(t, CHUNK - 1)).astype(BF16)
@@ -753,44 +753,45 @@
 
         return body
 
-    per_chunk([[(lambda: gather_1.line_b(1)), gather_2.line_b_own, (lambda: gather_1.line_a(0))], [(lambda: gather_1.line_b(2))], [(lambda: gather_2.line_a(0))], []], forward(0))
-    gather_1.line_b(0)
-    per_chunk([[], [(lambda: gather_1.twin(2))], [(lambda: gather_1.twin(1)), (lambda: gather_2.line_a(2)), (lambda: gather_1.twin(0)), (lambda: gather_2.line_a(1))], []], forward(1))
-    gather_2.line_b(0)
+    per_chunk([[(lambda: gather_1.line_b(0))], []], project, size=512)
+    gather_1.line_b(2)
+    per_chunk([[], [], [], []], forward(0))
+    per_chunk([[gather_1.line_b_own, (lambda: gather_2.line_a(1)), (lambda: gather_1.twin(0)), (lambda: gather_1.twin(1)), gather_2.line_b_own], [(lambda: gather_1.twin(2))], [], []], forward(1))
+    gather_2.line_a(2)
     gather_1.rest()
 
     c0 = 0.7978845608028654
     c1 = c0 * 0.044715
 
-    def hidden_units(which):
-        def body(t):
-            at = rows_of(t)
-            if which == 0:
-                after = n.inputs[at].astype(F32) + dot(n.context[at], weight(3))
-                centre = after - mean_last(after)
-                scale = lax.rsqrt(mean_last(centre * centre) + epsilon)
-                normal = centre * scale
-                n.normal_two[at] = normal.astype(BF16)
-                n.scale_two[at] = jnp.broadcast_to(scale, (CHUNK, 128))
-                normed = (normal * gain_two + shift_two).astype(BF16)
-                n.normed_ffn[at] = normed
-                n.result[at] = after + b_down
-            else:
-                normed = n.normed_ffn[at]
-            for i in (2 * which, 2 * which + 1):
-                pre = dot(normed, weight(4 + i)) + vecs[8 + i : 9 + i]
-                square = pre * pre
-                half = 0.5 + 0.5 * jnp.tanh(pre * (c0 + c1 * square))
-                hidden = pre * half
-                slope = half + (2.0 * hidden) * (1.0 - half) * (c0 + (3.0 * c1) * square)
-                cut = slice(i * WIDTH, (i + 1) * WIDTH)
-                n.hidden[at, cut] = hidden.astype(BF16)
-                n.grad_pre[at, cut] = slope.astype(BF16)
-
-        return body
-
-    per_chunk([[], [], [(lambda: gather_2.line_b(1))], []], hidden_units(0))
-    per_chunk([[(lambda: gather_2.line_b(2))], [], [], []], hidden_units(1))
+    def norm_two(t):
+        at = rows_of(t, 512)
+        after = n.inputs[at].astype(F32) + dot(n.context[at], weight(3))
+        centre = after - mean_last(after)
+        scale = lax.rsqrt(mean_last(centre * centre) + epsilon)
+        normal = centre * scale
+        n.normal_two[at] = normal.astype(BF16)
+        n.scale_two[at] = jnp.broadcast_to(scale, (512, 128))
+        n.normed_ffn[at] = (normal * gain_two + shift_two).astype(BF16)
+        n.result[at] = after + b_down
+
+    def hidden_units(i):
+        cut = slice(i * WIDTH, (i + 1) * WIDTH)
+        pre = dot(n.normed_ffn[...], weight(4 + i)) + vecs[8 + i : 9 + i]
+        square = pre * pre
+        half = 0.5 + 0.5 * jnp.tanh(pre * (c0 + c1 * square))
+        hidden = pre * half
+        slope = half + (2.0 * hidden) * (1.0 - half) * (c0 + (3.0 * c1) * square)
+        n.hidden[:, cut] = hidden.astype(BF16)
+        n.grad_pre[:, cut] = slope.astype(BF16)
+
+    per_chunk([[(lambda: gather_2.line_a(0))], []], norm_two, size=512)
+    hidden_units(0)
+    gather_2.line_b(1)
+    hidden_units(1)
+    gather_2.line_b(2)
+    hidden_units(2)
+    gather_2.line_b(0)
+    hidden_units(3)
     local[10].wait()
 
     def down_grads(i):
@@ -802,25 +803,24 @@
             )
 
     down_grads(0)
+    down_grads(1)
+    gather_2.twin(1)
     gather_2.twin(2)
-    down_grads(1)
     gather_2.twin(0)
-    gather_2.twin(1)
     down_grads(2)
     down_grads(3)
+    down_one.start()
     gather_2.rest()
 
-    def ffn(i, events):
+    def ffn(i):
         cut = slice(i * WIDTH, (i + 1) * WIDTH)
-
-        def body(t):
-            at = rows_of(t)
-            grad = dot_nt(n.cotangent[at], weight_down(i)) * n.grad_pre[at, cut].astype(F32)
-            grad = grad.astype(BF16)
-            n.grad_pre[at, cut] = grad
-            slots[0, i : i + 1] += column_sum(grad.astype(F32))
-
-        per_chunk(events, body)
+        grad = dot_nt(n.cotangent[...], weight_down(i)) * n.grad_pre[:, cut].astype(F32)
+        grad = grad.astype(BF16)
+        n.grad_pre[:, cut] = grad
+        slots[0, i : i + 1] += column_sum(grad.astype(F32))
+
+    def up_grads(i):
+        cut = slice(i * WIDTH, (i + 1) * WIDTH)
         for m in range(2):
             some = slice(m * 256, (m + 1) * 256)
             grad = dot_tn(n.normed_ffn[:, some], n.grad_pre[:, cut]).astype(BF16)
@@ -828,17 +828,22 @@
                 2, B, 2, R, WIDTH
             )
 
-    ffn(0, [[down_two.start], [], [], []])
-    down_one.start()
-    ffn(1, [[], [], [], []])
+    ffn(0)
+    up_grads(0)
+    down_two.start()
+    ffn(1)
+    up_grads(1)
+    down_one.after_core()
     up_one.start()
-    ffn(2, [[], [], [], [down_one.after_core]])
-    ffn(3, [[], [up_one.after_core], [], []])
+    down_two.after_core()
+    ffn(2)
+    up_grads(2)
+    ffn(3)
+    up_grads(3)
     up_two.start()
-    down_two.after_core()
 
     def norm_two_back(t):
-        at = rows_of(t)
+        at = rows_of(t, 512)
         grad = dot_nt(n.grad_pre[at, 0:WIDTH], weight(4))
         for i in range(1, 4):
             grad = grad + dot_nt(n.grad_pre[at, i * WIDTH : (i + 1) * WIDTH], weight(4 + i))
@@ -862,10 +867,11 @@
                 :, lanes[g]
             ]
 
-    per_chunk([[up_two.after_core], [], [], []], norm_two_back)
+    per_chunk([[up_one.after_core, up_two.after_core], []], norm_two_back, size=512)
     for m in range(2):
         grad = dot_tn(n.context[:, m * 256 : (m + 1) * 256], n.grad_attn[...]).astype(BF16)
         part[2 * m : 2 * m + 2, :, :, 3 * R : 4 * R, :] = grad.reshape(2, B, 2, R, WIDTH)
+    down_one.second()
 
     def backward(g):
         state_now[g] = jnp.zeros((GROUP, GROUP), F32)
@@ -912,19 +918,20 @@
             grad = dot_tn(n.normed_attn[...], ref[:, lanes[g]]).astype(BF16)
             part[:, :, :, i * R : (i + 1) * R, lanes[g]] = grad.reshape(A, B, 2, R, GROUP)
 
-    per_chunk([[], [down_one.second, out_all.start, up_one.second, down_two.second], [], []], backward(0), down=True)
+    per_chunk([[down_two.second, out_all.start], [], [], []], backward(0), down=True)
+    out_all.after_core()
     weight_grads(0)
     attn_one.start()
-    per_chunk([[up_one.third, attn_one.after_core, up_two.second], [down_two.third, down_one.third], [], []], backward(1), down=True)
+    per_chunk([[down_one.third, attn_one.after_core, up_one.second, down_two.third], [], [out_all.second], []], backward(1), down=True)
+    up_two.second()
     weight_grads(1)
+    up_one.third()
+    attn_three.start()
     attn_one.second()
-    out_all.after_core()
-    attn_three.start()
-    up_two.third()
     attn_two.start()
 
     def norm_one_back(t):
-        at = rows_of(t)
+        at = rows_of(t, 512)
         grad = dot_nt(n.grad_query[at], weight(0))
         grad = grad + dot_nt(n.grad_key[at], weight(1))
         grad = grad + dot_nt(n.grad_value[at], weight(2))
@@ -935,34 +942,30 @@
         back = e - mean_last(e) - normal * mean_last(e * normal)
         n.grad_normed[at] = n.grad_normed[at] + n.scale_one[at][:, 0:1] * back
 
-    per_chunk([[], [attn_three.after_core], [], []], norm_one_back)
+    per_chunk([[attn_two.after_core, attn_three.after_core, up_two.third], []], norm_one_back, size=512)
     store = pltpu.make_async_copy(n.grad_normed, n.grad_inputs_far, n.sem_local.at[11])
     store.start()
     T[0]()
-    attn_two.after_core()
-    out_all.second()
     attn_one.third()
     T[1]()
+    attn_two.second()
+    down_one.after_a()
     attn_three.second()
-    attn_two.second()
+    out_all.third()
 
     def outputs(t):
-        at = rows_of(t)
+        at = rows_of(t, 512)
         total = n.result[at]
         for i in range(4):
             total = total + dot(n.hidden[at, i * WIDTH : (i + 1) * WIDTH], weight_down(i))
         n.output[at] = total.astype(BF16)
 
-    per_chunk([[out_all.third, T[2], up_two.after_a, down_one.after_a, up_one.after_a, attn_two.third], [attn_three.third, T[3], out_all.after_a, attn_one.after_a], [], []], outputs)
+    per_chunk([[T[2], attn_two.third, attn_three.third, T[3], up_two.after_a, up_one.after_a, attn_one.after_a, down_one.finish, attn_two.after_a, up_one.finish, out_all.after_a, attn_three.after_a], []], outputs, size=512)
     store_more = pltpu.make_async_copy(n.output, n.output_far, n.sem_local.at[12])
     store_more.start()
-    attn_three.after_a()
-    down_one.finish()
-    up_one.finish()
     attn_one.finish()
+    attn_two.finish()
     out_all.finish()
-    attn_two.after_a()
-    up_two.finish()
     T[4]()
 
     total = slots[small_sum.now]
@@ -979,8 +982,8 @@
         picked = picked + jnp.where(keep, dot(high, pick) + dot(low, pick), 0.0)
     n.tiny_out[16:17] = column_sum(picked)
 
+    up_two.finish()
     attn_three.finish()
-    attn_two.finish()
     store.wait()
     store_more.wait()
     sends.finish()
@@ -1058,7 +1061,7 @@
     rows = 12 * R
     bits = max(reps.bit_length() - 2, 0)
     copies, n_slots = SmallReduce.counts(reps, shards)
-    sums = 5 * (2 * B + A + bits) + 2 * (3 * B - 1 + A + bits) + 1 * (3 * B - 1)
+    sums = 5 * (2 * B + A + bits) + 3 * (3 * B - 1 + A + bits) + 1 * (3 * B - 1)
     groups = 3
     w_query, w_key, w_value, w_out, w_up, w_down = weights
     b_up, b_down, gain_attn, shift_attn, gain_ffn, shift_ffn = vectors
@@ -1093,7 +1096,6 @@
     buffers = dict(
         inputs=(tall, BF16),
         cotangent=(tall, BF16),
-        output=(tall, BF16),
         result=(tall, F32),
         full=((A, B, 2, rows, WIDTH), BF16),
         part=((A, B, 2, rows, WIDTH), BF16),
@@ -1128,7 +1130,6 @@
         hidden=((length, 4 * WIDTH), BF16),
         grad_pre=((length, 4 * WIDTH), BF16),
         grad_normed=(tall, F32),
-        grad_attn=(tall, BF16),
         grad_mixed=(tall, BF16),
         grad_totals=(tall, F32),
     )
@@ -1147,6 +1148,7 @@
 
     def kernel(*refs):
         n = types.SimpleNamespace(**dict(zip(names, refs, strict=True)))
+        n.output, n.grad_attn = n.inputs, n.normed_ffn
         n.grad_query, n.grad_key, n.grad_value = (
             n.grad_pre.at[:, pl.ds(i * WIDTH, WIDTH)] for i in range(3)
         )

time: 105 us -> 99.3 us (0.946)
  Pallas kernels: 104 us -> 98.3 us
    pallas_call x1, Pallas kernels: 99.4 us -> 93.9 us  [layer(): pl.pallas_call(kernel, out_shape=tuple((jax.ShapeDtypeStruct(*spec) for s...]
where the time goes in v4:
time: 99.3 us; the launch traced here: 99.2 us
  Pallas kernels  98.3 us (99%)
    pallas_call x1, Pallas kernels, layer(): pl.pallas_call(kernel, out_shape=tuple((jax.ShapeDtypeStruct(*spec) for s...  93.9 us
    pallas_call x1, Pallas kernels, final(): pl.pallas_call(final_kernel, out_shape=tuple((jax.ShapeDtypeStruct(*shape...  4.42 us

profile of v4, /device:TPU:0, one launch (start us, length us, event | category | flops | bytes accessed | tf_op | source)
XLA Modules:
  0.0 99.2 jit_solution(17193277375510820728)
XLA Ops:
  0.7 93.9 %layer.1 = (bf16[1024,512]{1,0:T(8,128)(2,1)}, f32[1024,512]{1,0:T(8,128)}, bf16[384,512]{1,0:T(8,128)(2,1)}, f32[24,128]{1,0:T(8,128)}) custom-call(bf16[1024,512]{1,0:T(8,128)(2,1)} %bitcast.5, bf16[1024,512]{1,0:T(8,128)(2,1)} %bitcast.6, bf16[32,512]{1,0:T(8,128)(2,1)} %refs_2_.1, bf16[32,512]{1,0:T(8,128)(2,1)} %refs_3_.1, bf16[32,512]{1,0:T(8,128)(2,1)} %refs_4_.1, ...), custom_call_target="tpu_custom_call" | custom-call | flops 30064771072 | bytes 8388608 | tf_op jit(solution)/shard_map/layer/pallas_call | solution.py:1159
  94.6 4.4 %final.1 = (bf16[1024,512]{1,0:T(8,128)(2,1)}, f32[1024,512]{1,0:T(8,128)}, f32[32,512]{1,0:T(8,128)}, f32[32,512]{1,0:T(8,128)}, f32[32,512]{1,0:T(8,128)}, /*i...) custom-call(bf16[1024,512]{1,0:T(8,128)(2,1)} %get-tuple-element.32., ...), custom_call_target="tpu_custom_call" | custom-call | tf_op jit(solution)/shard_map/final/pallas_call | solution.py:1040

commit v5 on v4

--- a/solution.py
+++ b/solution.py
@@ -626,11 +626,11 @@
 
         lax.fori_loop(0, chunks, step, 0)
 
+    gather_0.own()
     tiny.own()
-    gather_0.own()
     tiny.second()
     gather_1.own()
-    gather_0.line_a(1)
+    tiny.third()
 
     seg_row = n.segment_ids[...].astype(F32)
     seg_rows = n.seg_rows
@@ -660,11 +660,16 @@
     def flags(one, two):
         return twice(jnp.where(one == two, 1.0, 0.0))
 
-    tiny.third()
+    gather_0.line_a(1)
+    tiny.last()
     gather_0.line_a(2)
-    tiny.last()
     gather_0.line_a(0)
     gather_0.line_b(1)
+    gather_0.line_b(2)
+    gather_0.line_b(0)
+    gather_1.line_a(1)
+    gather_0.line_b_own()
+    gather_1.line_a(2)
 
     local[9].wait()
     def norm_one(t):
@@ -676,15 +681,11 @@
         n.scale_one[at] = jnp.broadcast_to(scale, (CHUNK, 128))
 
     per_chunk([], norm_one)
-    gather_0.line_b(2)
-    gather_1.line_a(1)
     gather_0.twin(2)
     gather_1.line_a(0)
+    gather_0.twin(0)
     gather_0.twin(1)
-    gather_0.line_b(0)
-    gather_1.line_b(1)
-    gather_0.line_b_own()
-    gather_1.line_a(2)
+    gather_2.own()
 
     blocks = smalls[...].reshape(shards * 8, 128).astype(BF16)
     lane = iota((128, WIDTH), 1)
@@ -701,9 +702,8 @@
         vecs[8 + i : 9 + i] = jnp.sum(picked, axis=0)[0:1]
     b_down, gain_one, shift_one, gain_two, shift_two = (vecs[i : i + 1] for i in range(1, 6))
 
-    gather_2.own()
-    gather_0.twin(0)
     gather_0.rest()
+    gather_1.line_b(1)
 
     def weight(i):
         return full[:, :, :, i * R : (i + 1) * R, :].reshape(WIDTH, WIDTH)
@@ -753,11 +753,10 @@
 
         return body
 
-    per_chunk([[(lambda: gather_1.line_b(0))], []], project, size=512)
+    per_chunk([[], []], project, size=512)
     gather_1.line_b(2)
-    per_chunk([[], [], [], []], forward(0))
-    per_chunk([[gather_1.line_b_own, (lambda: gather_2.line_a(1)), (lambda: gather_1.twin(0)), (lambda: gather_1.twin(1)), gather_2.line_b_own], [(lambda: gather_1.twin(2))], [], []], forward(1))
-    gather_2.line_a(2)
+    per_chunk([[], [], [(lambda: gather_1.line_b(0))], []], forward(0))
+    per_chunk([[gather_2.line_b_own, (lambda: gather_2.line_a(0))], [(lambda: gather_1.twin(1))], [gather_1.line_b_own, (lambda: gather_1.twin(2)), (lambda: gather_1.twin(0)), (lambda: gather_2.line_a(1))], []], forward(1))
     gather_1.rest()
 
     c0 = 0.7978845608028654
@@ -784,13 +783,12 @@
         n.hidden[:, cut] = hidden.astype(BF16)
         n.grad_pre[:, cut] = slope.astype(BF16)
 
-    per_chunk([[(lambda: gather_2.line_a(0))], []], norm_two, size=512)
+    per_chunk([[(lambda: gather_2.line_a(2))], [(lambda: gather_2.line_b(0))]], norm_two, size=512)
     hidden_units(0)
     gather_2.line_b(1)
     hidden_units(1)
     gather_2.line_b(2)
     hidden_units(2)
-    gather_2.line_b(0)
     hidden_units(3)
     local[10].wait()
 
@@ -803,12 +801,13 @@
             )
 
     down_grads(0)
+    gather_2.twin(1)
+    gather_2.twin(0)
+    gather_2.twin(2)
     down_grads(1)
-    gather_2.twin(1)
-    gather_2.twin(2)
-    gather_2.twin(0)
     down_grads(2)
     down_grads(3)
+    down_two.start()
     down_one.start()
     gather_2.rest()
 
@@ -830,15 +829,14 @@
 
     ffn(0)
     up_grads(0)
-    down_two.start()
     ffn(1)
     up_grads(1)
-    down_one.after_core()
     up_one.start()
     down_two.after_core()
     ffn(2)
     up_grads(2)
     ffn(3)
+    down_one.after_core()
     up_grads(3)
     up_two.start()
 
@@ -867,11 +865,10 @@
                 :, lanes[g]
             ]
 
-    per_chunk([[up_one.after_core, up_two.after_core], []], norm_two_back, size=512)
+    per_chunk([[up_one.after_core], []], norm_two_back, size=512)
     for m in range(2):
         grad = dot_tn(n.context[:, m * 256 : (m + 1) * 256], n.grad_attn[...]).astype(BF16)
         part[2 * m : 2 * m + 2, :, :, 3 * R : 4 * R, :] = grad.reshape(2, B, 2, R, WIDTH)
-    down_one.second()
 
     def backward(g):
         state_now[g] = jnp.zeros((GROUP, GROUP), F32)
@@ -918,16 +915,17 @@
             grad = dot_tn(n.normed_attn[...], ref[:, lanes[g]]).astype(BF16)
             part[:, :, :, i * R : (i + 1) * R, lanes[g]] = grad.reshape(A, B, 2, R, GROUP)
 
-    per_chunk([[down_two.second, out_all.start], [], [], []], backward(0), down=True)
+    per_chunk([[down_two.second, down_one.second], [], [out_all.start, up_two.after_core], []], backward(0), down=True)
     out_all.after_core()
+    down_two.third()
     weight_grads(0)
     attn_one.start()
-    per_chunk([[down_one.third, attn_one.after_core, up_one.second, down_two.third], [], [out_all.second], []], backward(1), down=True)
+    per_chunk([[down_one.third, attn_one.after_core, up_one.second], [], [out_all.second], []], backward(1), down=True)
     up_two.second()
     weight_grads(1)
+    attn_one.second()
     up_one.third()
     attn_three.start()
-    attn_one.second()
     attn_two.start()
 
     def norm_one_back(t):
@@ -942,16 +940,17 @@
         back = e - mean_last(e) - normal * mean_last(e * normal)
         n.grad_normed[at] = n.grad_normed[at] + n.scale_one[at][:, 0:1] * back
 
-    per_chunk([[attn_two.after_core, attn_three.after_core, up_two.third], []], norm_one_back, size=512)
+    per_chunk([[attn_two.after_core, attn_three.after_core, out_all.third], []], norm_one_back, size=512)
     store = pltpu.make_async_copy(n.grad_normed, n.grad_inputs_far, n.sem_local.at[11])
     store.start()
+    up_two.third()
+    attn_one.third()
     T[0]()
-    attn_one.third()
     T[1]()
-    attn_two.second()
     down_one.after_a()
     attn_three.second()
-    out_all.third()
+    attn_two.second()
+    up_one.after_a()
 
     def outputs(t):
         at = rows_of(t, 512)
@@ -960,12 +959,18 @@
             total = total + dot(n.hidden[at, i * WIDTH : (i + 1) * WIDTH], weight_down(i))
         n.output[at] = total.astype(BF16)
 
-    per_chunk([[T[2], attn_two.third, attn_three.third, T[3], up_two.after_a, up_one.after_a, attn_one.after_a, down_one.finish, attn_two.after_a, up_one.finish, out_all.after_a, attn_three.after_a], []], outputs, size=512)
+    per_chunk([[attn_two.third, T[2], attn_three.third, up_one.finish, out_all.after_a, T[3], up_two.after_a], []], outputs, size=512)
     store_more = pltpu.make_async_copy(n.output, n.output_far, n.sem_local.at[12])
     store_more.start()
+    down_one.finish()
+    attn_two.after_a()
+    attn_one.after_a()
+    out_all.finish()
+    attn_three.after_a()
+    attn_two.finish()
+    attn_three.finish()
+    up_two.finish()
     attn_one.finish()
-    attn_two.finish()
-    out_all.finish()
     T[4]()
 
     total = slots[small_sum.now]
@@ -982,14 +987,12 @@
         picked = picked + jnp.where(keep, dot(high, pick) + dot(low, pick), 0.0)
     n.tiny_out[16:17] = column_sum(picked)
 
-    up_two.finish()
-    attn_three.finish()
     store.wait()
     store_more.wait()
     sends.finish()
 
 
-PIECES = 4
+PIECES = 2
 
 
 def final_kernel(output, grad_inputs, done, tiny, *refs):

time: 99.3 us -> 98.6 us (level)
  no operation moved by 1% of the time
where the time goes in v5:
time: 98.6 us; the launch traced here: 98.4 us
  Pallas kernels  97.6 us (99%)
    pallas_call x1, Pallas kernels, layer(): pl.pallas_call(kernel, out_shape=tuple((jax.ShapeDtypeStruct(*spec) for s...  93.4 us
    pallas_call x1, Pallas kernels, final(): pl.pallas_call(final_kernel, out_shape=tuple((jax.ShapeDtypeStruct(*shape...  4.22 us

profile of v5, /device:TPU:0, one launch (start us, length us, event | category | flops | bytes accessed | tf_op | source)
XLA Modules:
  0.0 98.4 jit_solution(13245957539530697926)
XLA Ops:
  0.7 93.4 %layer.1 = (bf16[1024,512]{1,0:T(8,128)(2,1)}, f32[1024,512]{1,0:T(8,128)}, bf16[384,512]{1,0:T(8,128)(2,1)}, f32[24,128]{1,0:T(8,128)}) custom-call(bf16[1024,512]{1,0:T(8,128)(2,1)} %bitcast.5, bf16[1024,512]{1,0:T(8,128)(2,1)} %bitcast.6, bf16[32,512]{1,0:T(8,128)(2,1)} %refs_2_.1, bf16[32,512]{1,0:T(8,128)(2,1)} %refs_3_.1, bf16[32,512]{1,0:T(8,128)(2,1)} %refs_4_.1, ...), custom_call_target="tpu_custom_call" | custom-call | flops 30064771072 | bytes 8388608 | tf_op jit(solution)/shard_map/layer/pallas_call | solution.py:1162
  94.0 4.2 %final.1 = (bf16[1024,512]{1,0:T(8,128)(2,1)}, f32[1024,512]{1,0:T(8,128)}, f32[32,512]{1,0:T(8,128)}, f32[32,512]{1,0:T(8,128)}, f32[32,512]{1,0:T(8,128)}, /*i...) custom-call(bf16[1024,512]{1,0:T(8,128)(2,1)} %get-tuple-element.32., ...), custom_call_target="tpu_custom_call" | custom-call | tf_op jit(solution)/shard_map/final/pallas_call | solution.py:1043

commit v6 on v5

--- a/solution.py
+++ b/solution.py
@@ -779,7 +779,7 @@
         square = pre * pre
         half = 0.5 + 0.5 * jnp.tanh(pre * (c0 + c1 * square))
         hidden = pre * half
-        slope = half + (2.0 * hidden) * (1.0 - half) * (c0 + (3.0 * c1) * square)
+        slope = half + hidden * (1.0 - half) * (2.0 * c0 + (6.0 * c1) * square)
         n.hidden[:, cut] = hidden.astype(BF16)
         n.grad_pre[:, cut] = slope.astype(BF16)
 

time: 98.6 us -> 98.4 us (level)
  no operation moved by 1% of the time
where the time goes in v6:
time: 98.4 us; the launch traced here: 98.2 us
  Pallas kernels  97.4 us (99%)
    pallas_call x1, Pallas kernels, layer(): pl.pallas_call(kernel, out_shape=tuple((jax.ShapeDtypeStruct(*spec) for s...  93.2 us
    pallas_call x1, Pallas kernels, final(): pl.pallas_call(final_kernel, out_shape=tuple((jax.ShapeDtypeStruct(*shape...  4.22 us

profile of v6, /device:TPU:0, one launch (start us, length us, event | category | flops | bytes accessed | tf_op | source)
XLA Modules:
  0.0 98.2 jit_solution(6345635706809236741)
XLA Ops:
  0.7 93.2 %layer.1 = (bf16[1024,512]{1,0:T(8,128)(2,1)}, f32[1024,512]{1,0:T(8,128)}, bf16[384,512]{1,0:T(8,128)(2,1)}, f32[24,128]{1,0:T(8,128)}) custom-call(bf16[1024,512]{1,0:T(8,128)(2,1)} %bitcast.5, bf16[1024,512]{1,0:T(8,128)(2,1)} %bitcast.6, bf16[32,512]{1,0:T(8,128)(2,1)} %refs_2_.1, bf16[32,512]{1,0:T(8,128)(2,1)} %refs_3_.1, bf16[32,512]{1,0:T(8,128)(2,1)} %refs_4_.1, ...), custom_call_target="tpu_custom_call" | custom-call | flops 30064771072 | bytes 8388608 | tf_op jit(solution)/shard_map/layer/pallas_call | solution.py:1162
  93.8 4.2 %final.1 = (bf16[1024,512]{1,0:T(8,128)(2,1)}, f32[1024,512]{1,0:T(8,128)}, f32[32,512]{1,0:T(8,128)}, f32[32,512]{1,0:T(8,128)}, f32[32,512]{1,0:T(8,128)}, /*i...) custom-call(bf16[1024,512]{1,0:T(8,128)(2,1)} %get-tuple-element.32., ...), custom_call_target="tpu_custom_call" | custom-call | tf_op jit(solution)/shard_map/final/pallas_call | solution.py:1043
